TPU v7x, 32 devices: a whole 2x2x4 slice. The times are simulated.
32 devices in a mesh: range: 4 (over x, core), azimuth: 8 (over z, y).
Axes of the slice: x: 2, y: 2, z: 4, core: 2. Of those that a mesh axis runs over, the one named last changes fastest.
Arguments:
- features: bfloat16 [4, 64, 64, 1024], P(None, None, 'range', 'azimuth'), may hold values from -6 to 6
- state_init: bfloat16 [64, 64, 1024], P(None, 'range', 'azimuth'), may hold values from -3 to 3
- kernel: float32 [64, 3, 3], replicated, may hold values from -2 to 2
- gate_weight: bfloat16 [128, 128], replicated, may hold values from -0.5 to 0.5
- cand_weight: bfloat16 [64, 64], replicated, may hold values from -0.75 to 0.75
- recur_weight: bfloat16 [64, 64], replicated, may hold values from -0.75 to 0.75
- down_weight: bfloat16 [128, 1024], replicated, may hold values from -0.1875 to 0.1875
- owner_map: int32 [4, 8, 4], P('range', 'azimuth'), may hold values from 0 to 3, as said below
- dest_map: int32 [4, 8, 4], P('range', 'azimuth'), may hold values from 0 to 3
- cart_cot: bfloat16 [4, 8, 4, 128, 128], P('range', 'azimuth'), may hold values from -6 to 6
Outputs:
- cart: float32 [4, 8, 4, 128, 128], P('range', 'azimuth')
- grad_features: bfloat16 [4, 64, 64, 1024], P(None, None, 'range', 'azimuth')
- grad_state: float32 [64, 64, 1024], P(None, 'range', 'azimuth')
- grad_kernel: float32 [64, 3, 3], replicated
- grad_gate: float32 [128, 128], replicated
- grad_cand: float32 [64, 64], replicated
- grad_recur: float32 [64, 64], replicated
- grad_down: float32 [128, 1024], replicated
Inputs may be any that keep to these rules, and one draw needn't show every extreme that they name: `owner_map`: no tile sends more than 2 of its 4 blocks to one owner; in every azimuth column one owner receives exactly 2 blocks from every tile of the column.
All inputs are finite; a program needn't handle non-finite values.
Results may differ from a plain program's by a relative error of at most 0.0065.
Values may be sent and summed in bfloat16 or wider, within the bound.
No kernel may reach another device: no remote copies, remote signals or barrier semaphores. Data moves between devices by JAX's collectives and lax.ppermute only.
A program may use at most 128 MiB of HBM per device.

v0:
```python
import math

import jax
import jax.numpy as jnp
from jax import lax
from jax.sharding import PartitionSpec as P

DILATION = 8


def extended(block, sides, width, periodic):
    for axis, dim in sides:
        count = lax.axis_size(axis)
        forward = [(i, i + 1) for i in range(count - 1)]
        if periodic:
            forward.append((count - 1, 0))
        backward = [(target, source) for source, target in forward]
        low = lax.ppermute(
            lax.slice_in_dim(block, block.shape[dim] - width, None, axis=dim), axis, forward
        )
        high = lax.ppermute(lax.slice_in_dim(block, 0, width, axis=dim), axis, backward)
        block = jnp.concatenate([low, block, high], axis=dim)
    return block


def depthwise(padded, kernel, tile_rows, tile_cols):
    summed = jnp.zeros((padded.shape[0], tile_rows, tile_cols), jnp.float32)
    for tap_row in range(3):
        for tap_col in range(3):
            window = padded[
                :,
                tap_row : tap_row + tile_rows,
                tap_col * DILATION : tap_col * DILATION + tile_cols,
            ]
            summed = summed + kernel[:, tap_row, tap_col][:, None, None] * window.astype(
                jnp.float32
            )
    return summed


def kernel_terms(padded, dconv, tile_rows, tile_cols):
    grads = dconv.astype(jnp.float32)
    outer_rows = []
    for tap_row in range(3):
        inner_cols = []
        for tap_col in range(3):
            window = padded[
                :,
                tap_row : tap_row + tile_rows,
                tap_col * DILATION : tap_col * DILATION + tile_cols,
            ]
            inner_cols.append(jnp.sum(grads * window.astype(jnp.float32), axis=(1, 2)))
        outer_rows.append(jnp.stack(inner_cols, axis=1))
    return jnp.stack(outer_rows, axis=1)


def patches(values, tile_rows, tile_cols):
    channels = values.shape[0]
    shaped = values.reshape(channels, tile_rows // 4, 4, tile_cols // 4, 4).transpose(0, 2, 4, 1, 3)
    return shaped.reshape(16 * channels, tile_rows * tile_cols // 16)


def unpatches(grads, tile_rows, tile_cols):
    channels = grads.shape[0] // 16
    shaped = grads.reshape(channels, 4, 4, tile_rows // 4, tile_cols // 4).transpose(0, 3, 1, 4, 2)
    return shaped.reshape(channels, tile_rows * tile_cols)


def cross_cells(left, right):
    return lax.dot_general(
        left, right, (((1,), (1,)), ((), ())), preferred_element_type=jnp.float32
    )


def back_product(weight, grads):
    return lax.dot_general(
        weight, grads, (((0,), (0,)), ((), ())), preferred_element_type=jnp.float32
    )


def cell_gates(conv_bf, prior_bf, gate_weight, cand_weight, recur_weight):
    channels = conv_bf.shape[0]
    stacked = jnp.concatenate([conv_bf, prior_bf], axis=0)
    preact = jnp.dot(gate_weight, stacked, preferred_element_type=jnp.float32)
    update = jax.nn.sigmoid(preact[:channels])
    reset = jax.nn.sigmoid(preact[channels:])
    recurrent = jnp.dot(recur_weight, prior_bf, preferred_element_type=jnp.float32)
    candidate = jnp.tanh(
        jnp.dot(cand_weight, conv_bf, preferred_element_type=jnp.float32) + reset * recurrent
    )
    return (stacked, update, reset, recurrent, candidate)


def reverse_cell(
    flow_grad,
    prior_state,
    update,
    reset,
    recurrent,
    candidate,
    gate_weight,
    cand_weight,
    recur_weight,
):
    channels = update.shape[0]
    d_update = flow_grad * (candidate - prior_state)
    d_act = flow_grad * update * (1.0 - candidate * candidate)
    d_recur = d_act * reset
    gate_delta = jnp.concatenate(
        [d_update * update * (1.0 - update), d_act * recurrent * reset * (1.0 - reset)], axis=0
    ).astype(jnp.bfloat16)
    cand_delta = d_act.astype(jnp.bfloat16)
    recur_delta = d_recur.astype(jnp.bfloat16)
    reverse_in = back_product(gate_weight, gate_delta)
    dconv = (reverse_in[:channels] + back_product(cand_weight, cand_delta)).astype(jnp.bfloat16)
    carry = (
        (1.0 - update) * flow_grad + reverse_in[channels:] + back_product(recur_weight, recur_delta)
    )
    return (carry, dconv, gate_delta, cand_delta, recur_delta)


def framed_each(field):
    taller = extended(field, (("range", 2),), 1, False)
    return extended(taller, (("azimuth", 3),), DILATION, True)


def on_device(
    features,
    state_init,
    kernel,
    gate_weight,
    cand_weight,
    recur_weight,
    down_weight,
    owner_map,
    dest_map,
    cart_cot,
):
    slice_count, channels, tile_rows, tile_cols = features.shape
    cell_count = tile_rows * tile_cols
    coarse_ch = down_weight.shape[0]
    rank_count = lax.axis_size("range")
    block_count = owner_map.shape[2]
    per_slice = block_count // slice_count
    block_cells = cell_count // 16 // per_slice
    capacity = block_count // 2
    hidden = state_init.reshape(channels, cell_count).astype(jnp.float32)
    padded_list = []
    conv_list = []
    hidden_list = [hidden]
    block_list = []
    for instant in range(slice_count):
        padded = framed_each(features[instant][None])[0]
        conv_bf = (
            depthwise(padded, kernel, tile_rows, tile_cols)
            .astype(jnp.bfloat16)
            .reshape(channels, cell_count)
        )
        stacked, update, reset, recurrent, candidate = cell_gates(
            conv_bf, hidden.astype(jnp.bfloat16), gate_weight, cand_weight, recur_weight
        )
        hidden = (1.0 - update) * hidden + update * candidate
        coarse = jnp.dot(
            down_weight,
            patches(hidden.astype(jnp.bfloat16), tile_rows, tile_cols),
            preferred_element_type=jnp.float32,
        ).astype(jnp.bfloat16)
        block_list.append(coarse.reshape(coarse_ch, per_slice, block_cells).transpose(1, 0, 2))
        padded_list.append(padded)
        conv_list.append(conv_bf)
        hidden_list.append(hidden)
    blocks = jnp.concatenate(block_list, axis=0).reshape(block_count, coarse_ch * block_cells)
    owners = owner_map[0, 0]
    targets = dest_map[0, 0]
    matches = (owners[None, :] == jnp.arange(rank_count, dtype=jnp.int32)[:, None]).astype(
        jnp.int32
    )
    position = jnp.cumsum(matches, axis=1) - matches
    picks = (matches[:, None, :] == 1) & (
        position[:, None, :] == jnp.arange(capacity, dtype=jnp.int32)[None, :, None]
    )
    pick_flat = picks.reshape(rank_count * capacity, block_count)
    outgoing = jnp.dot(
        pick_flat.astype(jnp.bfloat16), blocks, preferred_element_type=jnp.float32
    ).astype(jnp.bfloat16)
    outgoing = outgoing.reshape(rank_count, capacity, coarse_ch * block_cells)
    labels = jnp.sum(picks.astype(jnp.int32) * (targets[None, None, :] + 1), axis=2)
    arrived, arrived_labels = (
        lax.all_to_all(outgoing, "range", split_axis=0, concat_axis=0, tiled=True),
        lax.all_to_all(labels, "range", split_axis=0, concat_axis=0, tiled=True),
    )
    landing = (
        arrived_labels.reshape(1, rank_count * capacity) - 1
        == jnp.arange(block_count, dtype=jnp.int32)[:, None]
    ).astype(jnp.bfloat16)
    cartesian = jnp.dot(
        landing,
        arrived.reshape(rank_count * capacity, coarse_ch * block_cells),
        preferred_element_type=jnp.float32,
    )
    cartesian = cartesian.reshape(1, 1, block_count, coarse_ch, block_cells)
    cot_flat = cart_cot.reshape(block_count, coarse_ch * block_cells)
    replies = (
        back_product(landing, cot_flat)
        .astype(jnp.bfloat16)
        .reshape(rank_count, capacity, coarse_ch * block_cells)
    )
    returned = lax.all_to_all(replies, "range", split_axis=0, concat_axis=0, tiled=True)
    backed = back_product(
        pick_flat.astype(jnp.bfloat16),
        returned.reshape(rank_count * capacity, coarse_ch * block_cells),
    ).astype(jnp.bfloat16)
    carry = jnp.zeros((channels, cell_count), jnp.float32)
    grad_kernel = jnp.zeros((channels, 3, 3), jnp.float32)
    grad_gate = jnp.zeros((2 * channels, 2 * channels), jnp.float32)
    grad_cand = jnp.zeros((channels, channels), jnp.float32)
    grad_recur = jnp.zeros((channels, channels), jnp.float32)
    grad_down = jnp.zeros((coarse_ch, 16 * channels), jnp.float32)
    grad_list = [None] * slice_count
    flipped = kernel[:, ::-1, ::-1]
    for instant in range(slice_count - 1, -1, -1):
        prior_state = hidden_list[instant]
        prior_bf = prior_state.astype(jnp.bfloat16)
        conv_bf = conv_list[instant]
        stacked, update, reset, recurrent, candidate = cell_gates(
            conv_bf, prior_bf, gate_weight, cand_weight, recur_weight
        )
        next_bf = hidden_list[instant + 1].astype(jnp.bfloat16)
        slice_blocks = backed[instant * per_slice : (instant + 1) * per_slice].reshape(
            per_slice, coarse_ch, block_cells
        )
        d_coarse = slice_blocks.transpose(1, 0, 2).reshape(coarse_ch, per_slice * block_cells)
        grad_down = grad_down + cross_cells(d_coarse, patches(next_bf, tile_rows, tile_cols))
        flow_grad = carry + unpatches(back_product(down_weight, d_coarse), tile_rows, tile_cols)
        carry, dconv, gate_delta, cand_delta, recur_delta = reverse_cell(
            flow_grad,
            prior_state,
            update,
            reset,
            recurrent,
            candidate,
            gate_weight,
            cand_weight,
            recur_weight,
        )
        grad_gate = grad_gate + cross_cells(gate_delta, stacked)
        grad_cand = grad_cand + cross_cells(cand_delta, conv_bf)
        grad_recur = grad_recur + cross_cells(recur_delta, prior_bf)
        dconv_grid = dconv.reshape(channels, tile_rows, tile_cols)
        grad_kernel = grad_kernel + kernel_terms(
            padded_list[instant], dconv_grid, tile_rows, tile_cols
        )
        dpadded = framed_each(dconv_grid[None])[0]
        grad_list[instant] = depthwise(dpadded, flipped, tile_rows, tile_cols).astype(jnp.bfloat16)
    grad_kernel, grad_gate, grad_cand, grad_recur, grad_down = lax.psum(
        (grad_kernel, grad_gate, grad_cand, grad_recur, grad_down), ("range", "azimuth")
    )
    grad_scale = 1.0 / math.sqrt(slice_count * cell_count * rank_count * lax.axis_size("azimuth"))
    grad_features = jnp.stack(grad_list, axis=0)
    grad_state = carry.reshape(channels, tile_rows, tile_cols)
    return (
        cartesian,
        grad_features,
        grad_state,
        grad_kernel * grad_scale,
        grad_gate * grad_scale,
        grad_cand * grad_scale,
        grad_recur * grad_scale,
        grad_down * grad_scale,
    )


def solution(mesh):
    placed = (
        P(None, None, "range", "azimuth"),
        P(None, "range", "azimuth"),
        P(),
        P(),
        P(),
        P(),
        P(),
        P("range", "azimuth", None),
        P("range", "azimuth", None),
        P("range", "azimuth", None, None, None),
    )
    return jax.shard_map(
        on_device,
        mesh=mesh,
        in_specs=placed,
        out_specs=(
            P("range", "azimuth", None, None, None),
            P(None, None, "range", "azimuth"),
            P(None, "range", "azimuth"),
            P(),
            P(),
            P(),
            P(),
            P(),
        ),
        check_vma=False,
    )
```

profile of v0, /device:TPU:1, one launch (start us, length us, event | category | flops | bytes accessed | tf_op | source)
XLA Modules:
  0.0 493.9 jit_solution(7616606532913531842)
XLA Ops:
  10.2 4.3 all-to-all-start
  36.9 4.0 all-to-all-start.2
  55.4 4.2 collective-permute-start.3
  60.8 17.3 %collective-permute-done.6 = bf16[1,64,18,8]{3,2,1,0:T(8,128)(2,1)S(1)} collective-permute-done((bf16[1,64,18,8]{3,2,1,0:T(8,128)(2,1)S(1)}, bf16[1,64,18,8]{3,2,1,0:T(8,128)(2,1)S(1)}, u32[]{:S(2)}, u32[]{:S(2)}) %collective-permute-start.6) | collective-permute-done | bytes 18464 | tf_op jit(solution)/shard_map/ppermute | solution.py:18
  78.1 5.2 %collective-permute-start.15 = (bf16[1,64,18,8]{3,2,1,0:T(8,128)(2,1)}, bf16[1,64,18,8]{3,2,1,0:T(8,128)(2,1)}, u32[]{:S(2)}, u32[]{:S(2)}) collective-permute-start(bf16[1,64,18,8]{3,2,1,0:T(8,128)(2,1)} %get-tuple-element.119), channel_id=1, source_target_pairs={{1,0},{2,1},{3,2},{4,3},{5,4},{6,5},{7,6},{0,7},{9,8},{10,9},{11,1... | collective-permute-start | bytes 55304 | tf_op jit(solution)/shard_map/ppermute | solution.py:21
  83.4 5.4 %collective-permute-done.7 = bf16[1,64,18,8]{3,2,1,0:T(8,128)(2,1)S(1)} collective-permute-done((bf16[1,64,18,8]{3,2,1,0:T(8,128)(2,1)S(1)}, bf16[1,64,18,8]{3,2,1,0:T(8,128)(2,1)S(1)}, u32[]{:S(2)}, u32[]{:S(2)}) %collective-permute-start.7) | collective-permute-done | bytes 18464 | tf_op jit(solution)/shard_map/ppermute | solution.py:21
  88.7 6.2 %collective-permute-done.2 = bf16[1,64,18,8]{3,2,1,0:T(8,128)(2,1)S(1)} collective-permute-done((bf16[1,64,18,8]{3,2,1,0:T(8,128)(2,1)S(1)}, bf16[1,64,18,8]{3,2,1,0:T(8,128)(2,1)S(1)}, u32[]{:S(2)}, u32[]{:S(2)}) %collective-permute-start.2) | collective-permute-done | bytes 18464 | tf_op jit(solution)/shard_map/ppermute | solution.py:18
  95.0 5.3 %collective-permute-start.11 = (bf16[1,64,18,8]{3,2,1,0:T(8,128)(2,1)}, bf16[1,64,18,8]{3,2,1,0:T(8,128)(2,1)}, u32[]{:S(2)}, u32[]{:S(2)}) collective-permute-start(bf16[1,64,18,8]{3,2,1,0:T(8,128)(2,1)} %get-tuple-element.121), channel_id=1, source_target_pairs={{1,0},{2,1},{3,2},{4,3},{5,4},{6,5},{7,6},{0,7},{9,8},{10,9},{11,1... | collective-permute-start | bytes 55304 | tf_op jit(solution)/shard_map/ppermute | solution.py:21
  100.3 5.4 %collective-permute-done.3 = bf16[1,64,18,8]{3,2,1,0:T(8,128)(2,1)S(1)} collective-permute-done((bf16[1,64,18,8]{3,2,1,0:T(8,128)(2,1)S(1)}, bf16[1,64,18,8]{3,2,1,0:T(8,128)(2,1)S(1)}, u32[]{:S(2)}, u32[]{:S(2)}) %collective-permute-start.3) | collective-permute-done | bytes 18464 | tf_op jit(solution)/shard_map/ppermute | solution.py:21
  210.7 4.2 all-to-all-start.1
  219.9 3.7 collective-permute-start.28
  237.1 3.8 multiply_convert_fusion.5
  260.4 3.8 multiply_convert_fusion.2
  268.4 3.8 collective-permute-start.20
  281.2 3.7 multiply_convert_fusion
  296.1 38.0 %all-reduce = (f32[64,3,3]{0,2,1:T(4,128)S(1)}, f32[64,64]{1,0:T(8,128)S(1)}, f32[64,64]{1,0:T(8,128)S(1)}) all-reduce(f32[64,3,3]{0,2,1:T(4,128)S(1)} %fusion.173, f32[64,64]{1,0:T(8,128)S(1)} %convolution_add_fusion.9, f32[64,64]{1,0:T(8,128)S(1)} %convolution_add_fusion.6), channel_id=1, replica_groups=mesh['range'=4,'azimuth'=8] {'range','azimuth'}, use_global_device_ids=true, to_apply=%region_38.39 | all-reduce | flops 8768 | bytes 70144 | tf_op jit(solution)/shard_map/psum | solution.py:255
  340.3 3.8 collective-permute-start.16
  353.9 4.2 collective-permute-start.27
  358.6 15.9 %collective-permute-done.30 = bf16[1,64,18,8]{3,2,1,0:T(8,128)(2,1)S(1)} collective-permute-done((bf16[1,64,18,8]{3,2,1,0:T(8,128)(2,1)S(1)}, bf16[1,64,18,8]{3,2,1,0:T(8,128)(2,1)S(1)}, u32[]{:S(2)}, u32[]{:S(2)}) %collective-permute-start.30) | collective-permute-done | bytes 18464 | tf_op jit(solution)/shard_map/ppermute | solution.py:18
  374.6 4.2 collective-permute-start.23
  378.8 6.7 %collective-permute-done.31 = bf16[1,64,18,8]{3,2,1,0:T(8,128)(2,1)S(1)} collective-permute-done((bf16[1,64,18,8]{3,2,1,0:T(8,128)(2,1)S(1)}, bf16[1,64,18,8]{3,2,1,0:T(8,128)(2,1)S(1)}, u32[]{:S(2)}, u32[]{:S(2)}) %collective-permute-start.31) | collective-permute-done | bytes 18464 | tf_op jit(solution)/shard_map/ppermute | solution.py:21
  391.8 4.1 collective-permute-start.19
  395.9 7.0 %collective-permute-done.27 = bf16[1,64,18,8]{3,2,1,0:T(8,128)(2,1)S(1)} collective-permute-done((bf16[1,64,18,8]{3,2,1,0:T(8,128)(2,1)S(1)}, bf16[1,64,18,8]{3,2,1,0:T(8,128)(2,1)S(1)}, u32[]{:S(2)}, u32[]{:S(2)}) %collective-permute-start.27) | collective-permute-done | bytes 18464 | tf_op jit(solution)/shard_map/ppermute | solution.py:21
  425.3 57.9 %all-reduce.4.cloned.1.call-done = (f32[128,128]{1,0:T(8,128)}, f32[128,1024]{1,0:T(8,128)}) async-done(((f32[128,128]{1,0:T(8,128)}, f32[128,1024]{1,0:T(8,128)}), (f32[128,128]{1,0:T(8,128)}, f32[128,1024]{1,0:T(8,128)})) %all-reduce.4.cloned.1.call-update) | async-done | bytes 589840 | tf_op jit(solution)/shard_map/psum | solution.py:255
  (503 shorter events, 255.0 us)
Async XLA Ops:
  16.6 38.8 %collective-permute-start.12 = (bf16[1,64,1,128]{3,2,1,0:T(2,128)(2,1)S(1)}, bf16[1,64,1,128]{3,2,1,0:T(2,128)(2,1)S(1)}, u32[]{:S(2)}, u32[]{:S(2)}) collective-permute-start(bf16[1,64,1,128]{3,2,1,0:T(2,128)(2,1)S(1)} %get-tuple-element.98), channel_id=1, source_target_pairs={{0,8},{8,16},{16,24},{1,9},{9,17},{17,25},{2,10},{10,18},{18,26},{... | collective-permute-start | bytes 49160 | tf_op jit(solution)/shard_map/ppermute | solution.py:18
  20.2 29.1 %collective-permute-start.9 = (bf16[1,64,1,128]{3,2,1,0:T(2,128)(2,1)}, bf16[1,64,1,128]{3,2,1,0:T(2,128)(2,1)S(1)}, u32[]{:S(2)}, u32[]{:S(2)}) collective-permute-start(bf16[1,64,1,128]{3,2,1,0:T(2,128)(2,1)} %get-tuple-element.99), channel_id=1, source_target_pairs={{8,0},{16,8},{24,16},{9,1},{17,9},{25,17},{10,2},{18,10},{26,18},{... | collective-permute-start | bytes 49160 | tf_op jit(solution)/shard_map/ppermute | solution.py:21
  36.9 125.2 %all-to-all-start.2 = ((bf16[4,2,16384]{2,1,0:T(2,128)(2,1)}), bf16[4,2,16384]{2,1,0:T(2,128)(2,1)}, u32[]{:S(2)}, u32[]{:S(2)}) async-start(bf16[4,2,16384]{2,1,0:T(2,128)(2,1)} %reshape.271), calls=%async_computation.2 | async-start | bytes 524288 | tf_op jit(solution)/shard_map/all_to_all | solution.py:208
  50.7 27.5 %collective-permute-start.6 = (bf16[1,64,18,8]{3,2,1,0:T(8,128)(2,1)S(1)}, bf16[1,64,18,8]{3,2,1,0:T(8,128)(2,1)S(1)}, u32[]{:S(2)}, u32[]{:S(2)}) collective-permute-start(bf16[1,64,18,8]{3,2,1,0:T(8,128)(2,1)S(1)} %get-tuple-element.122), channel_id=1, source_target_pairs={{0,1},{1,2},{2,3},{3,4},{4,5},{5,6},{6,7},{7,0},{8,9},{9,10},{10,1... | collective-permute-start | bytes 55304 | tf_op jit(solution)/shard_map/ppermute | solution.py:18
  52.3 36.4 %collective-permute-start.7 = (bf16[1,64,18,8]{3,2,1,0:T(8,128)(2,1)S(1)}, bf16[1,64,18,8]{3,2,1,0:T(8,128)(2,1)S(1)}, u32[]{:S(2)}, u32[]{:S(2)}) collective-permute-start(bf16[1,64,18,8]{3,2,1,0:T(8,128)(2,1)S(1)} %get-tuple-element.123), channel_id=1, source_target_pairs={{1,0},{2,1},{3,2},{4,3},{5,4},{6,5},{7,6},{0,7},{9,8},{10,9},{11,1... | collective-permute-start | bytes 55304 | tf_op jit(solution)/shard_map/ppermute | solution.py:21
  55.4 39.6 %collective-permute-start.2 = (bf16[1,64,18,8]{3,2,1,0:T(8,128)(2,1)S(1)}, bf16[1,64,18,8]{3,2,1,0:T(8,128)(2,1)S(1)}, u32[]{:S(2)}, u32[]{:S(2)}) collective-permute-start(bf16[1,64,18,8]{3,2,1,0:T(8,128)(2,1)S(1)} %get-tuple-element.124), channel_id=1, source_target_pairs={{0,1},{1,2},{2,3},{3,4},{4,5},{5,6},{6,7},{7,0},{8,9},{9,10},{10,1... | collective-permute-start | bytes 55304 | tf_op jit(solution)/shard_map/ppermute | solution.py:18
  55.4 50.3 %collective-permute-start.3 = (bf16[1,64,18,8]{3,2,1,0:T(8,128)(2,1)S(1)}, bf16[1,64,18,8]{3,2,1,0:T(8,128)(2,1)S(1)}, u32[]{:S(2)}, u32[]{:S(2)}) collective-permute-start(bf16[1,64,18,8]{3,2,1,0:T(8,128)(2,1)S(1)} %get-tuple-element.125), channel_id=1, source_target_pairs={{1,0},{2,1},{3,2},{4,3},{5,4},{6,5},{7,6},{0,7},{9,8},{10,9},{11,1... | collective-permute-start | bytes 55304 | tf_op jit(solution)/shard_map/ppermute | solution.py:21
  60.8 56.5 %collective-permute-start.14 = (bf16[1,64,18,8]{3,2,1,0:T(8,128)(2,1)}, bf16[1,64,18,8]{3,2,1,0:T(8,128)(2,1)}, u32[]{:S(2)}, u32[]{:S(2)}) collective-permute-start(bf16[1,64,18,8]{3,2,1,0:T(8,128)(2,1)} %get-tuple-element.118), channel_id=1, source_target_pairs={{0,1},{1,2},{2,3},{3,4},{4,5},{5,6},{6,7},{7,0},{8,9},{9,10},{10,1... | collective-permute-start | bytes 55304 | tf_op jit(solution)/shard_map/ppermute | solution.py:18
  78.1 39.2 %collective-permute-start.15 = (bf16[1,64,18,8]{3,2,1,0:T(8,128)(2,1)}, bf16[1,64,18,8]{3,2,1,0:T(8,128)(2,1)}, u32[]{:S(2)}, u32[]{:S(2)}) collective-permute-start(bf16[1,64,18,8]{3,2,1,0:T(8,128)(2,1)} %get-tuple-element.119), channel_id=1, source_target_pairs={{1,0},{2,1},{3,2},{4,3},{5,4},{6,5},{7,6},{0,7},{9,8},{10,9},{11,1... | collective-permute-start | bytes 55304 | tf_op jit(solution)/shard_map/ppermute | solution.py:21
  88.7 30.2 %collective-permute-start.10 = (bf16[1,64,18,8]{3,2,1,0:T(8,128)(2,1)}, bf16[1,64,18,8]{3,2,1,0:T(8,128)(2,1)}, u32[]{:S(2)}, u32[]{:S(2)}) collective-permute-start(bf16[1,64,18,8]{3,2,1,0:T(8,128)(2,1)} %get-tuple-element.120), channel_id=1, source_target_pairs={{0,1},{1,2},{2,3},{3,4},{4,5},{5,6},{6,7},{7,0},{8,9},{9,10},{10,1... | collective-permute-start | bytes 55304 | tf_op jit(solution)/shard_map/ppermute | solution.py:18
  210.7 212.6 %all-to-all-start.1 = ((bf16[4,2,16384]{2,1,0:T(2,128)(2,1)}), bf16[4,2,16384]{2,1,0:T(2,128)(2,1)}, u32[]{:S(2)}, u32[]{:S(2)}) async-start(bf16[4,2,16384]{2,1,0:T(2,128)(2,1)} %reshape.268), calls=%async_computation.1 | async-start | bytes 524288 | tf_op jit(solution)/shard_map/all_to_all | solution.py:189
  214.9 268.3 %all-reduce.4.cloned.1.call-start = ((), (), s32[]{:S(2)}) async-start(), calls=%async_computation.3 | async-start | bytes 1179648 | tf_op jit(solution)/shard_map/psum | solution.py:255
  219.9 117.1 %collective-permute-start.28 = (bf16[1,64,1,128]{3,2,1,0:T(2,128)(2,1)}, bf16[1,64,1,128]{3,2,1,0:T(2,128)(2,1)}, u32[]{:S(2)}, u32[]{:S(2)}) collective-permute-start(bf16[1,64,1,128]{3,2,1,0:T(2,128)(2,1)} %get-tuple-element.132), channel_id=1, source_target_pairs={{0,8},{8,16},{16,24},{1,9},{9,17},{17,25},{2,10},{10,18},{18,26},{... | collective-permute-start | bytes 49160 | tf_op jit(solution)/shard_map/ppermute | solution.py:18
  223.6 116.8 %collective-permute-start.29 = (bf16[1,64,1,128]{3,2,1,0:T(2,128)(2,1)}, bf16[1,64,1,128]{3,2,1,0:T(2,128)(2,1)}, u32[]{:S(2)}, u32[]{:S(2)}) collective-permute-start(bf16[1,64,1,128]{3,2,1,0:T(2,128)(2,1)} %get-tuple-element.133), channel_id=1, source_target_pairs={{8,0},{16,8},{24,16},{9,1},{17,9},{25,17},{10,2},{18,10},{26,18},{... | collective-permute-start | bytes 49160 | tf_op jit(solution)/shard_map/ppermute | solution.py:21
  245.1 100.2 %collective-permute-start.24 = (bf16[1,64,1,128]{3,2,1,0:T(2,128)(2,1)}, bf16[1,64,1,128]{3,2,1,0:T(2,128)(2,1)}, u32[]{:S(2)}, u32[]{:S(2)}) collective-permute-start(bf16[1,64,1,128]{3,2,1,0:T(2,128)(2,1)} %get-tuple-element.130), channel_id=1, source_target_pairs={{0,8},{8,16},{16,24},{1,9},{9,17},{17,25},{2,10},{10,18},{18,26},{... | collective-permute-start | bytes 49160 | tf_op jit(solution)/shard_map/ppermute | solution.py:18
  248.8 98.5 %collective-permute-start.25 = (bf16[1,64,1,128]{3,2,1,0:T(2,128)(2,1)}, bf16[1,64,1,128]{3,2,1,0:T(2,128)(2,1)}, u32[]{:S(2)}, u32[]{:S(2)}) collective-permute-start(bf16[1,64,1,128]{3,2,1,0:T(2,128)(2,1)} %get-tuple-element.131), channel_id=1, source_target_pairs={{8,0},{16,8},{24,16},{9,1},{17,9},{25,17},{10,2},{18,10},{26,18},{... | collective-permute-start | bytes 49160 | tf_op jit(solution)/shard_map/ppermute | solution.py:21
  268.4 81.0 %collective-permute-start.20 = (bf16[1,64,1,128]{3,2,1,0:T(2,128)(2,1)}, bf16[1,64,1,128]{3,2,1,0:T(2,128)(2,1)}, u32[]{:S(2)}, u32[]{:S(2)}) collective-permute-start(bf16[1,64,1,128]{3,2,1,0:T(2,128)(2,1)} %get-tuple-element.128), channel_id=1, source_target_pairs={{0,8},{8,16},{16,24},{1,9},{9,17},{17,25},{2,10},{10,18},{18,26},{... | collective-permute-start | bytes 49160 | tf_op jit(solution)/shard_map/ppermute | solution.py:18
  349.4 36.0 %collective-permute-start.31 = (bf16[1,64,18,8]{3,2,1,0:T(8,128)(2,1)S(1)}, bf16[1,64,18,8]{3,2,1,0:T(8,128)(2,1)S(1)}, u32[]{:S(2)}, u32[]{:S(2)}) collective-permute-start(bf16[1,64,18,8]{3,2,1,0:T(8,128)(2,1)S(1)} %get-tuple-element.117), channel_id=1, source_target_pairs={{1,0},{2,1},{3,2},{4,3},{5,4},{6,5},{7,6},{0,7},{9,8},{10,9},{11,1... | collective-permute-start | bytes 55304 | tf_op jit(solution)/shard_map/ppermute | solution.py:21
  352.7 39.0 %collective-permute-start.26 = (bf16[1,64,18,8]{3,2,1,0:T(8,128)(2,1)S(1)}, bf16[1,64,18,8]{3,2,1,0:T(8,128)(2,1)S(1)}, u32[]{:S(2)}, u32[]{:S(2)}) collective-permute-start(bf16[1,64,18,8]{3,2,1,0:T(8,128)(2,1)S(1)} %get-tuple-element.114), channel_id=1, source_target_pairs={{0,1},{1,2},{2,3},{3,4},{4,5},{5,6},{6,7},{7,0},{8,9},{9,10},{10,1... | collective-permute-start | bytes 55304 | tf_op jit(solution)/shard_map/ppermute | solution.py:18
  353.9 48.9 %collective-permute-start.27 = (bf16[1,64,18,8]{3,2,1,0:T(8,128)(2,1)S(1)}, bf16[1,64,18,8]{3,2,1,0:T(8,128)(2,1)S(1)}, u32[]{:S(2)}, u32[]{:S(2)}) collective-permute-start(bf16[1,64,18,8]{3,2,1,0:T(8,128)(2,1)S(1)} %get-tuple-element.115), channel_id=1, source_target_pairs={{1,0},{2,1},{3,2},{4,3},{5,4},{6,5},{7,6},{0,7},{9,8},{10,9},{11,1... | collective-permute-start | bytes 55304 | tf_op jit(solution)/shard_map/ppermute | solution.py:21
  358.1 50.7 %collective-permute-start.22 = (bf16[1,64,18,8]{3,2,1,0:T(8,128)(2,1)S(1)}, bf16[1,64,18,8]{3,2,1,0:T(8,128)(2,1)S(1)}, u32[]{:S(2)}, u32[]{:S(2)}) collective-permute-start(bf16[1,64,18,8]{3,2,1,0:T(8,128)(2,1)S(1)} %get-tuple-element.112), channel_id=1, source_target_pairs={{0,1},{1,2},{2,3},{3,4},{4,5},{5,6},{6,7},{7,0},{8,9},{9,10},{10,1... | collective-permute-start | bytes 55304 | tf_op jit(solution)/shard_map/ppermute | solution.py:18
  374.6 37.2 %collective-permute-start.23 = (bf16[1,64,18,8]{3,2,1,0:T(8,128)(2,1)S(1)}, bf16[1,64,18,8]{3,2,1,0:T(8,128)(2,1)S(1)}, u32[]{:S(2)}, u32[]{:S(2)}) collective-permute-start(bf16[1,64,18,8]{3,2,1,0:T(8,128)(2,1)S(1)} %get-tuple-element.113), channel_id=1, source_target_pairs={{1,0},{2,1},{3,2},{4,3},{5,4},{6,5},{7,6},{0,7},{9,8},{10,9},{11,1... | collective-permute-start | bytes 55304 | tf_op jit(solution)/shard_map/ppermute | solution.py:21
  385.5 31.4 %collective-permute-start.18 = (bf16[1,64,18,8]{3,2,1,0:T(8,128)(2,1)S(1)}, bf16[1,64,18,8]{3,2,1,0:T(8,128)(2,1)S(1)}, u32[]{:S(2)}, u32[]{:S(2)}) collective-permute-start(bf16[1,64,18,8]{3,2,1,0:T(8,128)(2,1)S(1)} %get-tuple-element.110), channel_id=1, source_target_pairs={{0,1},{1,2},{2,3},{3,4},{4,5},{5,6},{6,7},{7,0},{8,9},{9,10},{10,1... | collective-permute-start | bytes 55304 | tf_op jit(solution)/shard_map/ppermute | solution.py:18
  391.8 28.3 %collective-permute-start.19 = (bf16[1,64,18,8]{3,2,1,0:T(8,128)(2,1)S(1)}, bf16[1,64,18,8]{3,2,1,0:T(8,128)(2,1)S(1)}, u32[]{:S(2)}, u32[]{:S(2)}) collective-permute-start(bf16[1,64,18,8]{3,2,1,0:T(8,128)(2,1)S(1)} %get-tuple-element.111), channel_id=1, source_target_pairs={{1,0},{2,1},{3,2},{4,3},{5,4},{6,5},{7,6},{0,7},{9,8},{10,9},{11,1... | collective-permute-start | bytes 55304 | tf_op jit(solution)/shard_map/ppermute | solution.py:21
  (144 other events, 2166.5 us)
Sparse Core Ops, SparseCore 0:
  337.0 146.1 all-reduce.3
where the time goes:
time: 502 us; the launch traced here: 494 us
  waiting for transfers between devices  140 us (28%)
  starting transfers between devices  95.3 us (19%)
  local copies, waits for them, and re-layouts  94.2 us (19%)
  matrix products  62.9 us (13%)
  other arithmetic  46.4 us (9%)
  blocking collectives  38 us (8%)
  between operations  16.7 us (3%)
    psum x1, waiting for transfers between devices, on_device(): lax.psum((grad_kernel, grad_gate, grad_cand, grad_recur, grad_down), ('ra...  57.9 us
    ppermute x16, starting transfers between devices, extended(): lax.ppermute(lax.slice_in_dim(block, 0, width, axis=dim), axis, backward)  50.7 us
    ppermute x16, waiting for transfers between devices, extended(): lax.ppermute(lax.slice_in_dim(block, block.shape[dim] - width, None, axis...  49.6 us
    psum x1, blocking collectives, on_device(): lax.psum((grad_kernel, grad_gate, grad_cand, grad_recur, grad_down), ('ra...  38 us
    ppermute x16, waiting for transfers between devices, extended(): lax.ppermute(lax.slice_in_dim(block, 0, width, axis=dim), axis, backward)  32.7 us
    ppermute x16, starting transfers between devices, extended(): lax.ppermute(lax.slice_in_dim(block, block.shape[dim] - width, None, axis...  32.2 us
    dot_general x18, matrix products, back_product(): lax.dot_general(weight, grads, (((0,), (0,)), ((), ())), preferred_elemen...  24.8 us
    dot_general x16, matrix products, cross_cells(): lax.dot_general(left, right, (((1,), (1,)), ((), ())), preferred_element_...  16.9 us
  transfers between devices with their start and end apart: 36, of which 15 were waited for; matrix products, arithmetic and copies ran while one was open for 29% of the time, Pallas kernels for 0%

commit v1 on v0

v1 whole, which is shorter than its diff:
```python
import functools
import math

import jax
import jax.numpy as jnp
import numpy as np
from jax import lax
from jax.experimental import pallas as pl
from jax.experimental.pallas import tpu as pltpu
from jax.sharding import PartitionSpec as P

DILATION = 8
LANES = 128
LABEL_ROWS = 16
F32 = jnp.float32
BF16 = jnp.bfloat16
NT = (((1,), (1,)), ((), ()))


def mm(left, right):
    return jnp.dot(left, right, preferred_element_type=F32)


def whole(shape):
    zeros = (0,) * len(shape)
    return pl.BlockSpec(shape, lambda *_: zeros)


def turn(value, shift):
    if isinstance(shift, int):
        shift = shift % LANES
        if shift == 0:
            return value
    return pltpu.roll(value, shift, 1)


def lane_index(shape):
    return lax.broadcasted_iota(jnp.int32, shape, len(shape) - 1)


def regroup(row_groups):
    cells = LANES // row_groups
    table = np.zeros((row_groups * LANES, 4 * LANES), np.float32)
    for group in range(row_groups):
        for col in range(LANES):
            phase, coarse = col % 4, col // 4
            table[group * LANES + col, phase * LANES + group * cells + coarse] = 1.0
    return table


def row_windows(row, edge_low, shift_low, edge_high, shift_high):
    lane = lane_index(row.shape)
    low = jnp.where(lane < DILATION, turn(edge_low, shift_low), turn(row, DILATION))
    high = jnp.where(
        lane >= LANES - DILATION, turn(edge_high, shift_high), turn(row, -DILATION)
    )
    return (low, row, high)


class Framed:
    def __init__(self, rows, body, low, high, top, top_edge, bottom, bottom_edge, step):
        self.rows = rows
        self.refs = (body, low, high, top, top_edge, bottom, bottom_edge)
        self.step = step

    def windows(self, start, size):
        body, low, high, top, top_edge, bottom, bottom_edge = self.refs
        span = pl.ds(start, size)
        edge_low = low[0, span, :].astype(F32)
        edge_high = high[0, span, :].astype(F32)
        base = self.step * (2 * DILATION)
        for row in range(-1, self.rows + 1):
            if 0 <= row < self.rows:
                value = body[0, row, span, :].astype(F32)
                yield row, row_windows(
                    value,
                    edge_low,
                    -DILATION * row,
                    edge_high,
                    LANES - DILATION - DILATION * row,
                )
            else:
                source, corner = (top, top_edge) if row < 0 else (bottom, bottom_edge)
                value = source[0, span, :].astype(F32)
                edge = corner[0, span, :].astype(F32)
                shift_low = (LANES - base) % LANES
                shift_high = (2 * LANES - 2 * DILATION - base) % LANES
                yield row, row_windows(value, edge, shift_low, edge, shift_high)


def depthwise_chunk(framed, start, size, taps, emit):
    sums = {}
    for row, windows in framed.windows(start, size):
        for above in range(3):
            target = row + 1 - above
            if not 0 <= target < framed.rows:
                continue
            for side in range(3):
                term = taps[3 * above + side] * windows[side]
                sums[target] = sums[target] + term if target in sums else term
        if row - 1 >= 0:
            emit(row - 1, sums.pop(row - 1))


def tap_columns(kernel_ref, start, size, flip):
    block = kernel_ref[pl.ds(start, size), :]
    order = [8 - tap if flip else tap for tap in range(9)]
    return [jnp.broadcast_to(block[:, tap : tap + 1], (size, LANES)) for tap in order]


def edge_columns(row_of, rows):
    low = high = None
    for row in range(rows):
        value = row_of(row)
        slot = lane_index(value.shape) // DILATION == row
        to_low = turn(value, DILATION * row)
        to_high = turn(value, DILATION * row + DILATION)
        low = jnp.where(slot, to_low, 0.0 if low is None else low)
        high = jnp.where(slot, to_high, 0.0 if high is None else high)
    return low.astype(BF16), high.astype(BF16)


def split_kernel(x_ref, rows_ref, low_ref, high_ref, flat):
    channels, rows = x_ref.shape[1], x_ref.shape[2]
    flat[...] = x_ref[0].reshape(channels * rows, LANES).astype(F32)

    def row_of(row):
        value = flat[pl.ds(row, channels, stride=rows), :]
        rows_ref[0, row] = value.astype(BF16)
        return value

    low_ref[0], high_ref[0] = edge_columns(row_of, rows)


def start_kernel(state_ref, table_ref, out_ref, flat):
    channels, rows = state_ref.shape[0], state_ref.shape[1]
    flat[...] = state_ref[...].reshape(channels * rows, LANES).astype(F32)
    for phase in range(4):
        parts = [
            flat[pl.ds(row, channels, stride=rows), :].astype(BF16)
            for row in range(phase, rows, 4)
        ]
        out_ref[phase * channels : (phase + 1) * channels, :] = mm(
            jnp.concatenate(parts, axis=1), table_ref[...]
        )


def message_kernel(first_ref, last_ref, low_ref, high_ref, down_ref, up_ref):
    slices = first_ref.shape[0]
    corner_down = corner_up = jnp.zeros(first_ref.shape[2:], F32)
    for step in range(slices):
        down_ref[step] = last_ref[step, 0]
        up_ref[step] = first_ref[step, 0]
        base = 2 * DILATION * step
        low = low_ref[step].astype(F32)
        high = high_ref[step].astype(F32)
        slot = lane_index(low.shape) // DILATION
        corner_down = jnp.where(slot == 2 * step, turn(low, base + DILATION), corner_down)
        corner_down = jnp.where(
            slot == 2 * step + 1, turn(high, base + 2 * DILATION), corner_down
        )
        corner_up = jnp.where(slot == 2 * step, turn(low, base), corner_up)
        corner_up = jnp.where(slot == 2 * step + 1, turn(high, base + DILATION), corner_up)
    down_ref[slices] = corner_down.astype(BF16)
    up_ref[slices] = corner_up.astype(BF16)


def forward_kernel(
    capacity,
    scale,
    owner_ref,
    dest_ref,
    x_ref,
    low_ref,
    high_ref,
    top_ref,
    top_edge_ref,
    bottom_ref,
    bottom_edge_ref,
    start_ref,
    kernel_ref,
    table_ref,
    weight_ref,
    down_ref,
    back_ref,
    out_ref,
    keep_ref,
    stack_ref,
    grad_down_ref,
    state,
    conv,
    patch,
):
    step = pl.program_id(0)
    slices = pl.num_programs(0)
    rows, channels = x_ref.shape[1], x_ref.shape[2]
    framed = Framed(
        rows,
        x_ref,
        low_ref,
        high_ref,
        top_ref,
        top_edge_ref,
        bottom_ref,
        bottom_edge_ref,
        step,
    )

    @pl.when(step == 0)
    def _():
        state[...] = start_ref[...]
        grad_down_ref[...] = jnp.zeros_like(grad_down_ref)
        out_ref[:, LANES:, :] = jnp.zeros_like(out_ref[:, LANES:, :])

    size = 16

    def conv_chunk(index, carry):
        start = pl.multiple_of(index * size, size)
        taps = tap_columns(kernel_ref, start, size, False)

        def emit(row, value):
            conv[row, pl.ds(start, size), :] = value.astype(BF16)

        depthwise_chunk(framed, start, size, taps, emit)
        return carry

    lax.fori_loop(0, channels // size, conv_chunk, 0)
    wide = jnp.concatenate(
        [
            jnp.concatenate([conv[row] for row in range(phase, rows, 4)], axis=1)
            for phase in range(4)
        ],
        axis=0,
    )
    grouped = mm(wide, table_ref[...]).astype(BF16)
    for phase in range(4):
        own = slice(phase * channels, (phase + 1) * channels)
        prior = state[own, :]
        stacked = jnp.concatenate([grouped[own], prior.astype(BF16)], axis=0)
        stack_ref[0, phase] = stacked
        pre = mm(weight_ref[...], stacked)
        signed_update = jnp.tanh(0.5 * pre[:channels])
        signed_reset = jnp.tanh(0.5 * pre[channels : 2 * channels])
        update = 0.5 + 0.5 * signed_update
        stay = 0.5 - 0.5 * signed_update
        reset = 0.5 + 0.5 * signed_reset
        recurrent = pre[3 * channels :]
        candidate = jnp.tanh(pre[2 * channels : 3 * channels] + reset * recurrent)
        following = stay * prior + update * candidate
        state[own, :] = following
        act = update * (1.0 - candidate * candidate)
        act_reset = act * reset
        keep_ref[0, 0, own, :] = (candidate - prior) * update * stay
        keep_ref[0, 1, own, :] = act_reset * recurrent * (0.5 - 0.5 * signed_reset)
        keep_ref[0, 2, own, :] = act
        keep_ref[0, 3, own, :] = act_reset
        keep_ref[0, 4, own, :] = stay
        rounded = following.astype(BF16).astype(F32)
        for col in range(4):
            patch[pl.ds(4 * phase + col, channels, stride=16), :] = rounded[
                :, col * LANES : (col + 1) * LANES
            ]
    patched = patch[...].astype(BF16)
    owner = owner_ref[step]
    position = jnp.int32(0)
    for earlier in range(owner_ref.shape[0]):
        position += jnp.where((earlier < step) & (owner_ref[earlier] == owner), 1, 0)
    slot = jnp.minimum(owner * capacity + position, out_ref.shape[0] - 1)
    out_ref[slot, :LANES, :] = mm(down_ref[...], patched).astype(BF16)
    label = (dest_ref[step] + 1).astype(F32)
    out_ref[slot, LANES:, :] = jnp.full((LABEL_ROWS, LANES), label, F32).astype(BF16)
    grad_down_ref[...] += lax.dot_general(
        back_ref[0], patched, NT, preferred_element_type=F32
    )

    @pl.when(step == slices - 1)
    def _():
        grad_down_ref[...] = grad_down_ref[...] * scale


def backward_kernel(
    scale,
    owner_ref,
    dest_ref,
    x_ref,
    low_ref,
    high_ref,
    top_ref,
    top_edge_ref,
    bottom_ref,
    bottom_edge_ref,
    keep_ref,
    stack_ref,
    back_ref,
    table_ref,
    weight_ref,
    down_ref,
    rows_ref,
    edge_low_ref,
    edge_high_ref,
    grad_state_ref,
    small_ref,
    carry,
    patch,
    dense,
    taps,
    flat,
):
    turn_index = pl.program_id(0)
    slices = pl.num_programs(0)
    step = slices - 1 - turn_index
    rows, channels = x_ref.shape[1], x_ref.shape[2]
    groups = rows // 4

    @pl.when(turn_index == 0)
    def _():
        carry[...] = jnp.zeros_like(carry)
        dense[...] = jnp.zeros_like(dense)
        taps[...] = jnp.zeros_like(taps)

    patch[...] = mm(down_ref[...], back_ref[0])
    flat_grads = []
    for phase in range(4):
        own = slice(phase * channels, (phase + 1) * channels)
        unpatched = jnp.concatenate(
            [patch[pl.ds(4 * phase + col, channels, stride=16), :] for col in range(4)], axis=1
        )
        flow = carry[own, :] + unpatched
        delta = jnp.concatenate(
            [(flow * keep_ref[0, part, own, :]).astype(BF16) for part in range(4)], axis=0
        )
        reverse = mm(weight_ref[...], delta)
        carry[own, :] = keep_ref[0, 4, own, :] * flow + reverse[channels:]
        flat_grads.append(reverse[:channels].astype(BF16))
        dense[...] += lax.dot_general(
            delta, stack_ref[0, phase], NT, preferred_element_type=F32
        )
    spread = mm(jnp.concatenate(flat_grads, axis=0), table_ref[...])

    def row_of(row):
        group, phase = row // 4, row % 4
        value = spread[
            phase * channels : (phase + 1) * channels, group * LANES : (group + 1) * LANES
        ]
        rows_ref[0, row] = value.astype(BF16)
        return value

    edge_low_ref[0], edge_high_ref[0] = edge_columns(row_of, rows)
    framed = Framed(
        rows,
        x_ref,
        low_ref,
        high_ref,
        top_ref,
        top_edge_ref,
        bottom_ref,
        bottom_edge_ref,
        step,
    )
    size = 16

    def tap_chunk(index, loop_carry):
        start = pl.multiple_of(index * size, size)
        span = pl.ds(start, size)
        sums = [taps[tap, span, :] for tap in range(9)]
        for row, windows in framed.windows(start, size):
            for above in range(3):
                target = row + 1 - above
                if not 0 <= target < rows:
                    continue
                grad = rows_ref[0, target, span, :].astype(F32)
                for side in range(3):
                    sums[3 * above + side] = sums[3 * above + side] + grad * windows[side]
        for tap in range(9):
            taps[tap, span, :] = sums[tap]
        return loop_carry

    lax.fori_loop(0, channels // size, tap_chunk, 0)

    @pl.when(turn_index == slices - 1)
    def _():
        remain = carry[...]
        total = None
        for _part in range(3):
            piece = remain.astype(BF16)
            remain = remain - piece.astype(F32)
            term = mm(piece, table_ref[...])
            total = term if total is None else total + term
        for phase in range(4):
            for group in range(groups):
                flat[pl.ds(4 * group + phase, channels, stride=rows), :] = total[
                    phase * channels : (phase + 1) * channels,
                    group * LANES : (group + 1) * LANES,
                ]
        grad_state_ref[...] = flat[...].reshape(channels, rows, LANES)
        small_ref[: 2 * channels, :] = dense[: 2 * channels, :] * scale
        lower = dense[2 * channels : 3 * channels, :]
        upper = dense[3 * channels :, :]
        small_ref[2 * channels : 3 * channels, :] = (
            jnp.where(lane_index(lower.shape) < channels, lower, upper) * scale
        )
        gathered = jnp.zeros((channels, LANES), F32)
        for tap in range(9):
            column = jnp.sum(taps[tap], axis=1, keepdims=True)
            gathered = jnp.where(lane_index(gathered.shape) == tap, column, gathered)
        small_ref[3 * channels :, :] = jnp.concatenate(
            [gathered.T[:16] * scale, jnp.zeros((16, LANES - channels), F32)], axis=1
        )


def features_kernel(
    x_ref,
    low_ref,
    high_ref,
    top_ref,
    top_edge_ref,
    bottom_ref,
    bottom_edge_ref,
    kernel_ref,
    out_ref,
    flat,
):
    step = pl.program_id(0)
    rows, channels = x_ref.shape[1], x_ref.shape[2]
    framed = Framed(
        rows,
        x_ref,
        low_ref,
        high_ref,
        top_ref,
        top_edge_ref,
        bottom_ref,
        bottom_edge_ref,
        step,
    )
    size = 16

    def conv_chunk(index, carry):
        start = pl.multiple_of(index * size, size)
        taps = tap_columns(kernel_ref, start, size, True)

        def emit(row, value):
            flat[pl.ds(start * rows + row, size, stride=rows), :] = value

        depthwise_chunk(framed, start, size, taps, emit)
        return carry

    lax.fori_loop(0, channels // size, conv_chunk, 0)
    out_ref[0] = flat[...].reshape(channels, rows, LANES).astype(BF16)


def landing_kernel(blocks, arrived_ref, out_ref):
    for dest in range(blocks):
        total = jnp.zeros(out_ref.shape[1:], F32)
        for slot in range(arrived_ref.shape[0]):
            label = arrived_ref[slot, LANES : LANES + LABEL_ROWS, :].astype(F32)[:1]
            value = arrived_ref[slot, :LANES, :].astype(F32)
            total = total + jnp.where(label == dest + 1, value, 0.0)
        out_ref[dest] = total


def finish_kernel(own_ref, other_ref, gate_ref, cand_ref, recur_ref, taps_ref):
    channels = cand_ref.shape[0]
    total = own_ref[...] + other_ref[...]
    gate_ref[...] = total[: 2 * channels]
    cand_ref[...] = total[2 * channels : 3 * channels, :channels]
    recur_ref[...] = total[2 * channels : 3 * channels, channels:]
    taps_ref[...] = total[3 * channels :, :channels].T


def shifted(value, axis, distance, periodic):
    count = lax.axis_size(axis)
    pairs = [(i, i + 1) for i in range(count - 1)]
    if periodic:
        pairs.append((count - 1, 0))
    if distance < 0:
        pairs = [(target, source) for source, target in pairs]
    return lax.ppermute(value, axis, pairs)


def frame_specs(slices, rows, channels, at):
    return [
        pl.BlockSpec((1, rows, channels, LANES), lambda i, *_: (at(i), 0, 0, 0)),
        pl.BlockSpec((1, channels, LANES), lambda i, *_: (at(i), 0, 0)),
        pl.BlockSpec((1, channels, LANES), lambda i, *_: (at(i), 0, 0)),
        pl.BlockSpec((1, channels, LANES), lambda i, *_: (at(i), 0, 0)),
        pl.BlockSpec((1, channels, LANES), lambda i, *_: (slices, 0, 0)),
        pl.BlockSpec((1, channels, LANES), lambda i, *_: (at(i), 0, 0)),
        pl.BlockSpec((1, channels, LANES), lambda i, *_: (slices, 0, 0)),
    ]


def exchange(rows_array, edge_low, edge_high):
    slices, rows, channels, _ = rows_array.shape
    low = shifted(edge_high, "azimuth", 1, True)
    high = shifted(edge_low, "azimuth", -1, True)
    message = jax.ShapeDtypeStruct((slices + 1, channels, LANES), BF16)
    row_block = (slices, 1, channels, LANES)
    down, up = pl.pallas_call(
        message_kernel,
        grid=(1,),
        in_specs=[
            pl.BlockSpec(row_block, lambda i: (0, 0, 0, 0)),
            pl.BlockSpec(row_block, lambda i: (0, rows - 1, 0, 0)),
            whole(low.shape),
            whole(high.shape),
        ],
        out_specs=[whole(message.shape)] * 2,
        out_shape=[message] * 2,
        name="message",
        cost_estimate=pl.CostEstimate(flops=1, bytes_accessed=1 << 20, transcendentals=0),
    )(rows_array, rows_array, low, high)
    top = shifted(down, "range", 1, False)
    bottom = shifted(up, "range", -1, False)
    return (rows_array, low, high, top, top, bottom, bottom)


def butterfly(value):
    pending = None
    for axis in ("range", "azimuth"):
        count = lax.axis_size(axis)
        gap = 1
        while gap < count:
            if pending is not None:
                value = value + pending
            pending = lax.ppermute(value, axis, [(i, i ^ gap) for i in range(count)])
            gap *= 2
    return value, pending


def on_device(
    features,
    state_init,
    kernel,
    gate_weight,
    cand_weight,
    recur_weight,
    down_weight,
    owner_map,
    dest_map,
    cart_cot,
):
    slices, channels, rows, cols = features.shape
    coarse_ch = down_weight.shape[0]
    ranks = lax.axis_size("range")
    sectors = lax.axis_size("azimuth")
    blocks = owner_map.shape[2]
    capacity = blocks // 2
    assert cols == LANES and rows * cols // 16 == LANES and blocks == slices
    scale = 1.0 / math.sqrt(slices * rows * cols * ranks * sectors)
    table = regroup(rows // 4)
    owners = owner_map.reshape(blocks)
    dests = dest_map.reshape(blocks)
    flat_scratch = pltpu.VMEM((channels * rows, LANES), F32)
    row_shape = jax.ShapeDtypeStruct((slices, rows, channels, LANES), BF16)
    edge_shape = jax.ShapeDtypeStruct((slices, channels, LANES), BF16)
    row_spec = pl.BlockSpec((1, rows, channels, LANES), lambda i, *_: (i, 0, 0, 0))
    edge_spec = pl.BlockSpec((1, channels, LANES), lambda i, *_: (i, 0, 0))
    arranged, edge_low, edge_high = pl.pallas_call(
        split_kernel,
        grid=(slices,),
        in_specs=[pl.BlockSpec((1, channels, rows, LANES), lambda i: (i, 0, 0, 0))],
        out_specs=[row_spec, edge_spec, edge_spec],
        out_shape=[row_shape, edge_shape, edge_shape],
        scratch_shapes=[flat_scratch],
        name="split",
        cost_estimate=pl.CostEstimate(flops=1, bytes_accessed=3 << 20, transcendentals=0),
    )(features)
    frame = exchange(arranged, edge_low, edge_high)

    cot = cart_cot.reshape(blocks, coarse_ch, LANES)
    cots = lax.all_to_all(
        jnp.broadcast_to(cot[None], (ranks,) + cot.shape), "range", 0, 0, tiled=True
    ).reshape(ranks * blocks, coarse_ch, LANES)

    group = (4 * channels, 4 * LANES)
    start = pl.pallas_call(
        start_kernel,
        in_specs=[pl.BlockSpec(memory_space=pltpu.VMEM)] * 2,
        out_specs=pl.BlockSpec(memory_space=pltpu.VMEM),
        out_shape=jax.ShapeDtypeStruct(group, F32),
        scratch_shapes=[flat_scratch],
        name="start",
        cost_estimate=pl.CostEstimate(flops=1 << 27, bytes_accessed=1 << 20, transcendentals=0),
    )(state_init, jnp.asarray(table, BF16))
    empty = jnp.zeros((channels, channels), BF16)
    weight = jnp.concatenate(
        [
            gate_weight,
            jnp.concatenate([cand_weight, empty], axis=1),
            jnp.concatenate([empty, recur_weight], axis=1),
        ],
        axis=0,
    )
    taps = kernel.reshape(channels, 9)
    back_spec = lambda at: pl.BlockSpec(
        (1, coarse_ch, LANES), lambda i, own, dst: (own[at(i)] * blocks + dst[at(i)], 0, 0)
    )
    ahead = lambda i: i
    behind = lambda i: slices - 1 - i
    out_blocks = jax.ShapeDtypeStruct((ranks * capacity, coarse_ch + LABEL_ROWS, LANES), BF16)
    keep_shape = jax.ShapeDtypeStruct((slices, 5) + group, F32)
    stack_shape = jax.ShapeDtypeStruct((slices, 4, 2 * channels, 4 * LANES), BF16)
    down_shape = jax.ShapeDtypeStruct(down_weight.shape, F32)
    keep_spec = lambda at: pl.BlockSpec((1, 5) + group, lambda i, *_: (at(i), 0, 0, 0))
    stack_spec = lambda at: pl.BlockSpec(
        (1, 4, 2 * channels, 4 * LANES), lambda i, *_: (at(i), 0, 0, 0)
    )
    outgoing, keep, stack, grad_down = pl.pallas_call(
        functools.partial(forward_kernel, capacity, scale),
        grid_spec=pltpu.PrefetchScalarGridSpec(
            num_scalar_prefetch=2,
            grid=(slices,),
            in_specs=frame_specs(slices, rows, channels, ahead)
            + [
                whole(group),
                whole(taps.shape),
                whole(table.shape),
                whole(weight.shape),
                whole(down_weight.shape),
                back_spec(ahead),
            ],
            out_specs=[
                whole(out_blocks.shape),
                keep_spec(ahead),
                stack_spec(ahead),
                whole(down_shape.shape),
            ],
            scratch_shapes=[
                pltpu.VMEM(group, F32),
                pltpu.VMEM((rows, channels, LANES), BF16),
                pltpu.VMEM((16 * channels, LANES), F32),
            ],
        ),
        out_shape=[out_blocks, keep_shape, stack_shape, down_shape],
        name="forward",
        cost_estimate=pl.CostEstimate(flops=1 << 30, bytes_accessed=16 << 20, transcendentals=0),
    )(
        owners,
        dests,
        *frame,
        start,
        taps,
        jnp.asarray(table, BF16),
        weight,
        down_weight,
        cots,
    )

    arrived = lax.all_to_all(
        outgoing.reshape((ranks, capacity) + outgoing.shape[1:]), "range", 0, 0, tiled=True
    ).reshape(outgoing.shape)
    shares = ranks * sectors
    sent = grad_down.astype(BF16).reshape(shares, coarse_ch * 16 * channels // (shares * LANES), LANES)
    pieces = lax.all_to_all(sent, ("range", "azimuth"), 0, 0, tiled=True)
    piece = jnp.sum(pieces.astype(F32), axis=0).astype(BF16)

    rows_grad, low_grad, high_grad, grad_state, small = pl.pallas_call(
        functools.partial(backward_kernel, scale),
        grid_spec=pltpu.PrefetchScalarGridSpec(
            num_scalar_prefetch=2,
            grid=(slices,),
            in_specs=frame_specs(slices, rows, channels, behind)
            + [
                keep_spec(behind),
                stack_spec(behind),
                back_spec(behind),
                whole(table.T.shape),
                whole(weight.T.shape),
                whole(down_weight.T.shape),
            ],
            out_specs=[
                pl.BlockSpec((1, rows, channels, LANES), lambda i, *_: (behind(i), 0, 0, 0)),
                pl.BlockSpec((1, channels, LANES), lambda i, *_: (behind(i), 0, 0)),
                pl.BlockSpec((1, channels, LANES), lambda i, *_: (behind(i), 0, 0)),
                whole((channels, rows, LANES)),
                whole((3 * channels + 16, LANES)),
            ],
            scratch_shapes=[
                pltpu.VMEM(group, F32),
                pltpu.VMEM((16 * channels, LANES), F32),
                pltpu.VMEM((4 * channels, 2 * channels), F32),
                pltpu.VMEM((9, channels, LANES), F32),
                flat_scratch,
            ],
        ),
        out_shape=[
            row_shape,
            edge_shape,
            edge_shape,
            jax.ShapeDtypeStruct((channels, rows, LANES), F32),
            jax.ShapeDtypeStruct((3 * channels + 16, LANES), F32),
        ],
        name="backward",
        cost_estimate=pl.CostEstimate(flops=1 << 30, bytes_accessed=16 << 20, transcendentals=0),
    )(
        owners,
        dests,
        *frame,
        keep,
        stack,
        cots,
        jnp.asarray(table.T, BF16),
        weight.T,
        down_weight.T,
    )

    cartesian = pl.pallas_call(
        functools.partial(landing_kernel, blocks),
        in_specs=[pl.BlockSpec(memory_space=pltpu.VMEM)],
        out_specs=pl.BlockSpec(memory_space=pltpu.VMEM),
        out_shape=jax.ShapeDtypeStruct((blocks, coarse_ch, LANES), F32),
        name="landing",
        cost_estimate=pl.CostEstimate(flops=1, bytes_accessed=1 << 19, transcendentals=0),
    )(arrived)
    spread = lax.all_to_all(
        jnp.broadcast_to(piece[None], sent.shape), ("range", "azimuth"), 0, 0, tiled=True
    )
    grad_down = spread.astype(F32).reshape(down_weight.shape)

    frame_grad = exchange(rows_grad, low_grad, high_grad)
    grad_features = pl.pallas_call(
        features_kernel,
        grid=(slices,),
        in_specs=frame_specs(slices, rows, channels, ahead) + [whole(taps.shape)],
        out_specs=pl.BlockSpec((1, channels, rows, LANES), lambda i: (i, 0, 0, 0)),
        out_shape=jax.ShapeDtypeStruct(features.shape, BF16),
        scratch_shapes=[flat_scratch],
        name="features",
        cost_estimate=pl.CostEstimate(flops=1 << 25, bytes_accessed=4 << 20, transcendentals=0),
    )(*frame_grad, taps)

    own, other = butterfly(small)
    grad_gate, grad_cand, grad_recur, grad_taps = pl.pallas_call(
        finish_kernel,
        in_specs=[pl.BlockSpec(memory_space=pltpu.VMEM)] * 2,
        out_specs=[pl.BlockSpec(memory_space=pltpu.VMEM)] * 4,
        out_shape=[
            jax.ShapeDtypeStruct((2 * channels, 2 * channels), F32),
            jax.ShapeDtypeStruct((channels, channels), F32),
            jax.ShapeDtypeStruct((channels, channels), F32),
            jax.ShapeDtypeStruct((channels, 16), F32),
        ],
        name="finish",
        cost_estimate=pl.CostEstimate(flops=1, bytes_accessed=1 << 18, transcendentals=0),
    )(own, other)
    return (
        cartesian.reshape(cart_cot.shape),
        grad_features,
        grad_state,
        grad_taps[:, :9].reshape(channels, 3, 3),
        grad_gate,
        grad_cand,
        grad_recur,
        grad_down,
    )


def solution(mesh):
    placed = (
        P(None, None, "range", "azimuth"),
        P(None, "range", "azimuth"),
        P(),
        P(),
        P(),
        P(),
        P(),
        P("range", "azimuth", None),
        P("range", "azimuth", None),
        P("range", "azimuth", None, None, None),
    )
    return jax.shard_map(
        on_device,
        mesh=mesh,
        in_specs=placed,
        out_specs=(
            P("range", "azimuth", None, None, None),
            P(None, None, "range", "azimuth"),
            P(None, "range", "azimuth"),
            P(),
            P(),
            P(),
            P(),
            P(),
        ),
        check_vma=False,
    )
```

time: 502 us -> 131 us (0.26); the launches traced: 494 us -> 130 us
  waiting for transfers between devices: 140 us -> 21.9 us
  local copies, waits for them, and re-layouts: 94.2 us -> 14.6 us
  matrix products: 62.9 us -> 0 us
  starting transfers between devices: 95.3 us -> 45 us
  Pallas kernels: 0 us -> 45 us
  other arithmetic: 46.4 us -> 2.87 us
  blocking collectives: 38 us -> 0 us
  between operations: 16.7 us -> 0.84 us
    ppermute x32 -> x13, waiting for transfers between devices: 82.3 us -> 12.6 us  [the longest x5 6.49 us: butterfly(): pending = lax.ppermute(value, axis, [(i, i ^ gap) for i in range(count)])]
    dot_general x52 -> x0, matrix products: 62.9 us -> none  [the longest x18 24.8 us: back_product(): lax.dot_general(weight, grads, (((0,), (0,)), ((), ())), preferred_elemen...]
    psum x1 -> x0, waiting for transfers between devices: 57.9 us -> none  [on_device(): lax.psum((grad_kernel, grad_gate, grad_cand, grad_recur, grad_down), ('ra...]
    ppermute x32 -> x13, starting transfers between devices: 82.9 us -> 29 us  [the longest x8 23.4 us: shifted(): return lax.ppermute(value, axis, pairs)]
    pallas_call x0 -> x9, Pallas kernels: none -> 45 us  [the longest x1 13.4 us: on_device(): pl.pallas_call(functools.partial(forward_kernel, capacity, scale), grid_s...]
    psum x1 -> x0, blocking collectives: 38 us -> none  [on_device(): lax.psum((grad_kernel, grad_gate, grad_cand, grad_recur, grad_down), ('ra...]
    reshape x15 -> x5, local copies, waits for them, and re-layouts: 32 us -> 3.74 us  [the longest x2 1.41 us: on_device(): taps = kernel.reshape(channels, 9)]
    transpose x8 -> x0, local copies, waits for them, and re-layouts: 25 us -> none  [the longest x4 13.9 us: patches(): values.reshape(channels, tile_rows // 4, 4, tile_cols // 4, 4)]
  transfers between devices with their start and end apart: 36 -> 17, of which waited for: 15 -> 6; matrix products, arithmetic and copies ran while one was open for 29% -> 7% of each run, Pallas kernels for 0% -> 24%
where the time goes in v1:
time: 131 us; the launch traced here: 130 us
  starting transfers between devices  45 us (34%)
  Pallas kernels  45 us (34%)
  waiting for transfers between devices  21.9 us (17%)
  local copies, waits for them, and re-layouts  14.6 us (11%)
  other arithmetic  2.87 us (2%)
    ppermute x8, starting transfers between devices, shifted(): return lax.ppermute(value, axis, pairs)  23.4 us
    pallas_call x1, Pallas kernels, on_device(): pl.pallas_call(functools.partial(forward_kernel, capacity, scale), grid_s...  13.4 us
    pallas_call x1, Pallas kernels, on_device(): pl.pallas_call(functools.partial(backward_kernel, scale), grid_spec=pltpu...  13.1 us
    all_to_all x1, waiting for transfers between devices, on_device(): pieces = lax.all_to_all(sent, ('range', 'azimuth'), 0, 0, tiled=True)  9.28 us
    unnamed x30, local copies, waits for them, and re-layouts  6.7 us
    ppermute x5, waiting for transfers between devices, butterfly(): pending = lax.ppermute(value, axis, [(i, i ^ gap) for i in range(count)])  6.49 us
    ppermute x8, waiting for transfers between devices, shifted(): return lax.ppermute(value, axis, pairs)  6.15 us
    ppermute x5, starting transfers between devices, butterfly(): pending = lax.ppermute(value, axis, [(i, i ^ gap) for i in range(count)])  5.62 us
  transfers between devices with their start and end apart: 17, of which 6 were waited for; matrix products, arithmetic and copies ran while one was open for 7% of the time, Pallas kernels for 24%

profile of v1, /device:TPU:1, one launch (start us, length us, event | category | flops | bytes accessed | tf_op | source)
XLA Modules:
  0.0 130.2 jit_solution(9633269447543382553)
XLA Ops:
  0.6 1.8 %broadcast_in_dim.7 = bf16[4,4,128,128]{3,2,1,0:T(8,128)(2,1)} broadcast(bf16[4,128,128]{2,1,0:T(8,128)(2,1)} %bitcast.21), dimensions={1,2,3} | broadcast | bytes 655360 | tf_op jit(solution)/shard_map/broadcast_in_dim | solution.py:573
  2.5 4.3 %all-to-all-start = ((bf16[4,4,128,128]{3,2,1,0:T(8,128)(2,1)}), bf16[4,4,128,128]{3,2,1,0:T(8,128)(2,1)S(1)}, u32[]{:S(2)}, u32[]{:S(2)}) async-start(bf16[4,4,128,128]{3,2,1,0:T(8,128)(2,1)} %broadcast_in_dim.7), calls=%async_computation | async-start | bytes 1048576 | tf_op jit(solution)/shard_map/all_to_all | solution.py:572
  6.7 3.7 %split.1 = (bf16[4,16,64,128]{3,2,1,0:T(8,128)(2,1)}, bf16[4,64,128]{2,1,0:T(8,128)(2,1)}, bf16[4,64,128]{2,1,0:T(8,128)(2,1)}) custom-call(bf16[4,64,16,128]{3,2,1,0:T(8,128)(2,1)} %x_ref.1), custom_call_target="tpu_custom_call" | custom-call | flops 1 | bytes 3145728 | tf_op jit(solution)/shard_map/split/pallas_call | solution.py:559
  10.5 1.9 %collective-permute-start = (bf16[4,64,128]{2,1,0:T(8,128)(2,1)}, bf16[4,64,128]{2,1,0:T(8,128)(2,1)S(1)}, u32[]{:S(2)}, u32[]{:S(2)}) collective-permute-start(bf16[4,64,128]{2,1,0:T(8,128)(2,1)} %get-tuple-element.29), channel_id=1, source_target_pairs={{0,1},{1,2},{2,3},{3,4},{4,5},{5,6},{6,7},{7,0},{8,9},{9,10},{10,1... | collective-permute-start | bytes 196616 | tf_op jit(solution)/shard_map/ppermute | solution.py:478
  12.4 3.1 %collective-permute-start.1 = (bf16[4,64,128]{2,1,0:T(8,128)(2,1)}, bf16[4,64,128]{2,1,0:T(8,128)(2,1)S(1)}, u32[]{:S(2)}, u32[]{:S(2)}) collective-permute-start(bf16[4,64,128]{2,1,0:T(8,128)(2,1)} %get-tuple-element.30), channel_id=1, source_target_pairs={{1,0},{2,1},{3,2},{4,3},{5,4},{6,5},{7,6},{0,7},{9,8},{10,9},{11,1... | collective-permute-start | bytes 196616 | tf_op jit(solution)/shard_map/ppermute | solution.py:478
  20.1 1.7 %message.2 = (bf16[5,64,128]{2,1,0:T(8,128)(2,1)}, bf16[5,64,128]{2,1,0:T(8,128)(2,1)}) custom-call(bf16[4,16,64,128]{3,2,1,0:T(8,128)(2,1)} %get-tuple-element.28.first_ref.last_ref.x_ref, bf16[4,16,64,128]{3,2,1,0:T(8,128)(2,1)} %get-tuple-element.28.first_ref.last_ref.x_ref, bf16[4,64,128]{2,1,0:T(8,128)(2,1)} %copy-done.7, bf16[4,64,128]{2,1,0:T(8,128)(2,1)} %copy-done.8), custom_call_target="tpu_custom_call" | custom-call | flops 1 | bytes 1048576 | tf_op jit(solution)/shard_map/message/pallas_call | solution.py:499
  21.8 3.8 %collective-permute-start.2 = (bf16[5,64,128]{2,1,0:T(8,128)(2,1)}, bf16[5,64,128]{2,1,0:T(8,128)(2,1)S(1)}, u32[]{:S(2)}, u32[]{:S(2)}) collective-permute-start(bf16[5,64,128]{2,1,0:T(8,128)(2,1)} %get-tuple-element.31), channel_id=1, source_target_pairs={{0,8},{8,16},{16,24},{1,9},{9,17},{17,25},{2,10},{10,18},{18,26},{... | collective-permute-start | bytes 245768 | tf_op jit(solution)/shard_map/ppermute | solution.py:478
  25.6 1.9 %collective-permute-start.3 = (bf16[5,64,128]{2,1,0:T(8,128)(2,1)}, bf16[5,64,128]{2,1,0:T(8,128)(2,1)S(1)}, u32[]{:S(2)}, u32[]{:S(2)}) collective-permute-start(bf16[5,64,128]{2,1,0:T(8,128)(2,1)} %get-tuple-element.32), channel_id=1, source_target_pairs={{8,0},{16,8},{24,16},{9,1},{17,9},{25,17},{10,2},{18,10},{26,18},{... | collective-permute-start | bytes 245768 | tf_op jit(solution)/shard_map/ppermute | solution.py:478
  28.3 2.4 %start.1.start_ref = f32[256,512]{1,0:T(8,128)} custom-call(bf16[64,16,128]{2,1,0:T(8,128)(2,1)} %state_ref.1, bf16[512,512]{1,0:T(8,128)(2,1)} %constant.8.clone.table_ref), custom_call_target="tpu_custom_call" | custom-call | flops 134217728 | bytes 1048576 | tf_op jit(solution)/shard_map/start/pallas_call | solution.py:577
  32.4 13.4 %forward.1 = (bf16[8,144,128]{2,1,0:T(8,128)(2,1)}, f32[4,5,256,512]{3,2,1,0:T(8,128)}, bf16[4,4,128,512]{3,2,1,0:T(8,128)(2,1)}, f32[128,1024]{1,0:T(8,128)}) custom-call(s32[4]{0:T(128)} %bitcast.23, s32[4]{0:T(128)} %bitcast.25, bf16[4,16,64,128]{3,2,1,0:T(8,128)(2,1)} %get-tuple-element.28.first_ref.last_ref.x_ref, bf16[4,64,128]{2,1,0:T(8,128)(2,1)} %copy-done.7, ...), custom_call_target="tpu_custom_call" | custom-call | flops 1073741824 | bytes 16777216 | tf_op jit(solution)/shard_map/forward/pallas_call | solution.py:609
  47.7 4.1 %all-to-all-start.2 = ((bf16[32,32,128]{2,1,0:T(8,128)(2,1)}), bf16[32,32,128]{2,1,0:T(8,128)(2,1)S(1)}, u32[]{:S(2)}, u32[]{:S(2)}) async-start(bf16[32,32,128]{2,1,0:T(8,128)(2,1)} %reshape.59), calls=%async_computation.2 | async-start | bytes 524288 | tf_op jit(solution)/shard_map/all_to_all | solution.py:655
  52.6 9.3 %all-to-all-done.2 = bf16[32,32,128]{2,1,0:T(8,128)(2,1)S(1)} async-done(((bf16[32,32,128]{2,1,0:T(8,128)(2,1)}), bf16[32,32,128]{2,1,0:T(8,128)(2,1)S(1)}, u32[]{:S(2)}, u32[]{:S(2)}) %all-to-all-start.2) | async-done | bytes 262176 | tf_op jit(solution)/shard_map/all_to_all | solution.py:655
  61.9 4.0 %all-to-all-start.1 = ((bf16[4,2,144,128]{3,2,1,0:T(8,128)(2,1)}), bf16[4,2,144,128]{3,2,1,0:T(8,128)(2,1)S(1)}, u32[]{:S(2)}, u32[]{:S(2)}) async-start(bf16[4,2,144,128]{3,2,1,0:T(8,128)(2,1)} %bitcast.19), calls=%async_computation.1 | async-start | bytes 589824 | tf_op jit(solution)/shard_map/all_to_all | solution.py:650
  66.6 13.1 %backward.1 = (bf16[4,16,64,128]{3,2,1,0:T(8,128)(2,1)}, bf16[4,64,128]{2,1,0:T(8,128)(2,1)}, bf16[4,64,128]{2,1,0:T(8,128)(2,1)}, f32[64,16,128]{2,1,0:T(8,128)}, f32[208,128]{1,0:T(8,128)}) custom-call(s32[4]{0:T(128)} %bitcast.24, s32[4]{0:T(128)} %bitcast.26, bf16[4,16,64,128]{3,2,1,0:T(8,128)(2,1)} %get-tuple-element.28.first_ref.last_ref.x_ref, ...), custom_call_target="tpu_custom_call" | custom-call | flops 1073741824 | bytes 16777216 | tf_op jit(solution)/shard_map/backward/pallas_call | solution.py:658
  80.7 3.7 %all-to-all-start.3 = ((bf16[32,32,128]{2,1,0:T(8,128)(2,1)}), bf16[32,32,128]{2,1,0:T(8,128)(2,1)S(1)}, u32[]{:S(2)}, u32[]{:S(2)}) async-start(bf16[32,32,128]{2,1,0:T(8,128)(2,1)} %broadcast_in_dim.16), calls=%async_computation.3 | async-start | bytes 524288 | tf_op jit(solution)/shard_map/all_to_all | solution.py:716
  86.7 4.2 %collective-permute-done.9 = f32[208,128]{1,0:T(8,128)S(1)} collective-permute-done((f32[208,128]{1,0:T(8,128)S(1)}, f32[208,128]{1,0:T(8,128)S(1)}, u32[]{:S(2)}, u32[]{:S(2)}) %collective-permute-start.9) | collective-permute-done | bytes 106528 | tf_op jit(solution)/shard_map/ppermute | solution.py:526
  92.4 2.3 %collective-permute-done.10 = f32[208,128]{1,0:T(8,128)S(1)} collective-permute-done((f32[208,128]{1,0:T(8,128)S(1)}, f32[208,128]{1,0:T(8,128)S(1)}, u32[]{:S(2)}, u32[]{:S(2)}) %collective-permute-start.10) | collective-permute-done | bytes 106528 | tf_op jit(solution)/shard_map/ppermute | solution.py:526
  97.4 2.9 %collective-permute-start.5 = (bf16[4,64,128]{2,1,0:T(8,128)(2,1)}, bf16[4,64,128]{2,1,0:T(8,128)(2,1)S(1)}, u32[]{:S(2)}, u32[]{:S(2)}) collective-permute-start(bf16[4,64,128]{2,1,0:T(8,128)(2,1)} %get-tuple-element.38), channel_id=1, source_target_pairs={{1,0},{2,1},{3,2},{4,3},{5,4},{6,5},{7,6},{0,7},{9,8},{10,9},{11,1... | collective-permute-start | bytes 196616 | tf_op jit(solution)/shard_map/ppermute | solution.py:478
  103.4 1.7 %message.3 = (bf16[5,64,128]{2,1,0:T(8,128)(2,1)}, bf16[5,64,128]{2,1,0:T(8,128)(2,1)}) custom-call(bf16[4,16,64,128]{3,2,1,0:T(8,128)(2,1)} %get-tuple-element.36.first_ref.last_ref.x_ref, bf16[4,16,64,128]{3,2,1,0:T(8,128)(2,1)} %get-tuple-element.36.first_ref.last_ref.x_ref, bf16[4,64,128]{2,1,0:T(8,128)(2,1)} %copy-done.9, bf16[4,64,128]{2,1,0:T(8,128)(2,1)} %copy-done.10), custom_call_target="tpu_custom_call" | custom-call | flops 1 | bytes 1048576 | tf_op jit(solution)/shard_map/message/pallas_call | solution.py:499
  105.2 6.5 %collective-permute-start.6 = (bf16[5,64,128]{2,1,0:T(8,128)(2,1)}, bf16[5,64,128]{2,1,0:T(8,128)(2,1)S(1)}, u32[]{:S(2)}, u32[]{:S(2)}) collective-permute-start(bf16[5,64,128]{2,1,0:T(8,128)(2,1)} %get-tuple-element.39), channel_id=1, source_target_pairs={{0,8},{8,16},{16,24},{1,9},{9,17},{17,25},{2,10},{10,18},{18,26},{... | collective-permute-start | bytes 245768 | tf_op jit(solution)/shard_map/ppermute | solution.py:478
  111.7 1.9 %collective-permute-start.7 = (bf16[5,64,128]{2,1,0:T(8,128)(2,1)}, bf16[5,64,128]{2,1,0:T(8,128)(2,1)S(1)}, u32[]{:S(2)}, u32[]{:S(2)}) collective-permute-start(bf16[5,64,128]{2,1,0:T(8,128)(2,1)} %get-tuple-element.40), channel_id=1, source_target_pairs={{8,0},{16,8},{24,16},{9,1},{17,9},{25,17},{10,2},{18,10},{26,18},{... | collective-permute-start | bytes 245768 | tf_op jit(solution)/shard_map/ppermute | solution.py:478
  113.7 4.0 %collective-permute-done.7.bottom_ref.bottom_edge_ref = bf16[5,64,128]{2,1,0:T(8,128)(2,1)S(1)} collective-permute-done((bf16[5,64,128]{2,1,0:T(8,128)(2,1)}, bf16[5,64,128]{2,1,0:T(8,128)(2,1)S(1)}, u32[]{:S(2)}, u32[]{:S(2)}) %collective-permute-start.7) | collective-permute-done | bytes 81952 | tf_op jit(solution)/shard_map/ppermute | solution.py:478
  118.3 5.3 %features.1 = bf16[4,64,16,128]{3,2,1,0:T(8,128)(2,1)} custom-call(bf16[4,16,64,128]{3,2,1,0:T(8,128)(2,1)} %get-tuple-element.36.first_ref.last_ref.x_ref, bf16[4,64,128]{2,1,0:T(8,128)(2,1)} %copy-done.9, bf16[4,64,128]{2,1,0:T(8,128)(2,1)} %copy-done.10, bf16[5,64,128]{2,1,0:T(8,128)(2,1)} %copy-done.3, bf16[5,64,128]{2,1,0:T(8,128)(2,1)} %copy-done.3, ...), custom_call_target="tpu_custom_call" | custom-call | flops 33554432 | bytes 4194304 | tf_op jit(solution)/shard_map/features/pallas_call | solution.py:722
  123.7 1.9 %landing.1 = f32[4,128,128]{2,1,0:T(8,128)} custom-call(bf16[8,144,128]{2,1,0:T(8,128)(2,1)} %bitcast.17), custom_call_target="tpu_custom_call" | custom-call | flops 1 | bytes 524288 | tf_op jit(solution)/shard_map/landing/pallas_call | solution.py:708
  (66 shorter events, 26.4 us)
Async XLA Ops:
  0.6 51.1 %copy-start.11 = (bf16[128,1024]{1,0:T(8,128)(2,1)S(1)}, bf16[128,1024]{1,0:T(8,128)(2,1)}, u32[]{:S(2)}) copy-start(bf16[128,1024]{1,0:T(8,128)(2,1)} %down_ref.1) | copy-start | bytes 786436
  2.5 29.1 %all-to-all-start = ((bf16[4,4,128,128]{3,2,1,0:T(8,128)(2,1)}), bf16[4,4,128,128]{3,2,1,0:T(8,128)(2,1)S(1)}, u32[]{:S(2)}, u32[]{:S(2)}) async-start(bf16[4,4,128,128]{3,2,1,0:T(8,128)(2,1)} %broadcast_in_dim.7), calls=%async_computation | async-start | bytes 1048576 | tf_op jit(solution)/shard_map/all_to_all | solution.py:572
  10.5 8.9 %collective-permute-start = (bf16[4,64,128]{2,1,0:T(8,128)(2,1)}, bf16[4,64,128]{2,1,0:T(8,128)(2,1)S(1)}, u32[]{:S(2)}, u32[]{:S(2)}) collective-permute-start(bf16[4,64,128]{2,1,0:T(8,128)(2,1)} %get-tuple-element.29), channel_id=1, source_target_pairs={{0,1},{1,2},{2,3},{3,4},{4,5},{5,6},{6,7},{7,0},{8,9},{9,10},{10,1... | collective-permute-start | bytes 196616 | tf_op jit(solution)/shard_map/ppermute | solution.py:478
  12.4 7.0 %collective-permute-start.1 = (bf16[4,64,128]{2,1,0:T(8,128)(2,1)}, bf16[4,64,128]{2,1,0:T(8,128)(2,1)S(1)}, u32[]{:S(2)}, u32[]{:S(2)}) collective-permute-start(bf16[4,64,128]{2,1,0:T(8,128)(2,1)} %get-tuple-element.30), channel_id=1, source_target_pairs={{1,0},{2,1},{3,2},{4,3},{5,4},{6,5},{7,6},{0,7},{9,8},{10,9},{11,1... | collective-permute-start | bytes 196616 | tf_op jit(solution)/shard_map/ppermute | solution.py:478
  21.8 8.9 %collective-permute-start.2 = (bf16[5,64,128]{2,1,0:T(8,128)(2,1)}, bf16[5,64,128]{2,1,0:T(8,128)(2,1)S(1)}, u32[]{:S(2)}, u32[]{:S(2)}) collective-permute-start(bf16[5,64,128]{2,1,0:T(8,128)(2,1)} %get-tuple-element.31), channel_id=1, source_target_pairs={{0,8},{8,16},{16,24},{1,9},{9,17},{17,25},{2,10},{10,18},{18,26},{... | collective-permute-start | bytes 245768 | tf_op jit(solution)/shard_map/ppermute | solution.py:478
  25.6 6.0 %collective-permute-start.3 = (bf16[5,64,128]{2,1,0:T(8,128)(2,1)}, bf16[5,64,128]{2,1,0:T(8,128)(2,1)S(1)}, u32[]{:S(2)}, u32[]{:S(2)}) collective-permute-start(bf16[5,64,128]{2,1,0:T(8,128)(2,1)} %get-tuple-element.32), channel_id=1, source_target_pairs={{8,0},{16,8},{24,16},{9,1},{17,9},{25,17},{10,2},{18,10},{26,18},{... | collective-permute-start | bytes 245768 | tf_op jit(solution)/shard_map/ppermute | solution.py:478
  30.7 0.9 copy-start.5
  31.6 0.8 copy-start
  47.7 14.2 %all-to-all-start.2 = ((bf16[32,32,128]{2,1,0:T(8,128)(2,1)}), bf16[32,32,128]{2,1,0:T(8,128)(2,1)S(1)}, u32[]{:S(2)}, u32[]{:S(2)}) async-start(bf16[32,32,128]{2,1,0:T(8,128)(2,1)} %reshape.59), calls=%async_computation.2 | async-start | bytes 524288 | tf_op jit(solution)/shard_map/all_to_all | solution.py:655
  61.9 18.0 %all-to-all-start.1 = ((bf16[4,2,144,128]{3,2,1,0:T(8,128)(2,1)}), bf16[4,2,144,128]{3,2,1,0:T(8,128)(2,1)S(1)}, u32[]{:S(2)}, u32[]{:S(2)}) async-start(bf16[4,2,144,128]{3,2,1,0:T(8,128)(2,1)} %bitcast.19), calls=%async_computation.1 | async-start | bytes 589824 | tf_op jit(solution)/shard_map/all_to_all | solution.py:650
  79.7 4.7 %collective-permute-start.8 = (f32[208,128]{1,0:T(8,128)}, f32[208,128]{1,0:T(8,128)S(1)}, u32[]{:S(2)}, u32[]{:S(2)}) collective-permute-start(f32[208,128]{1,0:T(8,128)} %get-tuple-element.42), channel_id=1, source_target_pairs={{0,8},{8,0},{16,24},{24,16},{1,9},{9,1},{17,25},{25,17},{2,10},{10... | collective-permute-start | bytes 319496 | tf_op jit(solution)/shard_map/ppermute | solution.py:526
  79.9 43.8 %copy-start.1 = (bf16[4,2,144,128]{3,2,1,0:T(8,128)(2,1)}, bf16[4,2,144,128]{3,2,1,0:T(8,128)(2,1)S(1)}, u32[]{:S(2)}) copy-start(bf16[4,2,144,128]{3,2,1,0:T(8,128)(2,1)S(1)} %all-to-all-done.1) | copy-start | bytes 884740
  80.7 48.7 %all-to-all-start.3 = ((bf16[32,32,128]{2,1,0:T(8,128)(2,1)}), bf16[32,32,128]{2,1,0:T(8,128)(2,1)S(1)}, u32[]{:S(2)}, u32[]{:S(2)}) async-start(bf16[32,32,128]{2,1,0:T(8,128)(2,1)} %broadcast_in_dim.16), calls=%async_computation.3 | async-start | bytes 524288 | tf_op jit(solution)/shard_map/all_to_all | solution.py:716
  85.3 5.6 %collective-permute-start.9 = (f32[208,128]{1,0:T(8,128)S(1)}, f32[208,128]{1,0:T(8,128)S(1)}, u32[]{:S(2)}, u32[]{:S(2)}) collective-permute-start(f32[208,128]{1,0:T(8,128)S(1)} %add.16), channel_id=1, source_target_pairs={{0,16},{8,24},{16,0},{24,8},{1,17},{9,25},{17,1},{25,9},{2,18},{10... | collective-permute-start | bytes 319496 | tf_op jit(solution)/shard_map/ppermute | solution.py:526
  90.9 3.8 %collective-permute-start.10 = (f32[208,128]{1,0:T(8,128)S(1)}, f32[208,128]{1,0:T(8,128)S(1)}, u32[]{:S(2)}, u32[]{:S(2)}) collective-permute-start(f32[208,128]{1,0:T(8,128)S(1)} %add.17), channel_id=1, source_target_pairs={{0,1},{1,0},{2,3},{3,2},{4,5},{5,4},{6,7},{7,6},{8,9},{9,8},{10,11... | collective-permute-start | bytes 319496 | tf_op jit(solution)/shard_map/ppermute | solution.py:526
  94.7 5.5 %collective-permute-start.11 = (f32[208,128]{1,0:T(8,128)S(1)}, f32[208,128]{1,0:T(8,128)S(1)}, u32[]{:S(2)}, u32[]{:S(2)}) collective-permute-start(f32[208,128]{1,0:T(8,128)S(1)} %add.18), channel_id=1, source_target_pairs={{0,2},{1,3},{2,0},{3,1},{4,6},{5,7},{6,4},{7,5},{8,10},{9,11},{10,... | collective-permute-start | bytes 319496 | tf_op jit(solution)/shard_map/ppermute | solution.py:526
  96.1 6.7 %collective-permute-start.4 = (bf16[4,64,128]{2,1,0:T(8,128)(2,1)}, bf16[4,64,128]{2,1,0:T(8,128)(2,1)S(1)}, u32[]{:S(2)}, u32[]{:S(2)}) collective-permute-start(bf16[4,64,128]{2,1,0:T(8,128)(2,1)} %get-tuple-element.37), channel_id=1, source_target_pairs={{0,1},{1,2},{2,3},{3,4},{4,5},{5,6},{6,7},{7,0},{8,9},{9,10},{10,1... | collective-permute-start | bytes 196616 | tf_op jit(solution)/shard_map/ppermute | solution.py:478
  97.4 5.4 %collective-permute-start.5 = (bf16[4,64,128]{2,1,0:T(8,128)(2,1)}, bf16[4,64,128]{2,1,0:T(8,128)(2,1)S(1)}, u32[]{:S(2)}, u32[]{:S(2)}) collective-permute-start(bf16[4,64,128]{2,1,0:T(8,128)(2,1)} %get-tuple-element.38), channel_id=1, source_target_pairs={{1,0},{2,1},{3,2},{4,3},{5,4},{6,5},{7,6},{0,7},{9,8},{10,9},{11,1... | collective-permute-start | bytes 196616 | tf_op jit(solution)/shard_map/ppermute | solution.py:478
  100.3 25.2 %copy-start.2 = (f32[208,128]{1,0:T(8,128)}, f32[208,128]{1,0:T(8,128)S(1)}, u32[]{:S(2)}) copy-start(f32[208,128]{1,0:T(8,128)S(1)} %add.19.own_ref) | copy-start | bytes 319492
  100.3 25.2 %collective-permute-start.12 = (f32[208,128]{1,0:T(8,128)S(1)}, f32[208,128]{1,0:T(8,128)S(1)}, u32[]{:S(2)}, u32[]{:S(2)}) collective-permute-start(f32[208,128]{1,0:T(8,128)S(1)} %add.19.own_ref), channel_id=1, source_target_pairs={{0,4},{1,5},{2,6},{3,7},{4,0},{5,1},{6,2},{7,3},{8,12},{9,13},{10,... | collective-permute-start | bytes 319496 | tf_op jit(solution)/shard_map/ppermute | solution.py:526
  102.8 0.6 copy-start.10
  105.2 8.5 %collective-permute-start.6 = (bf16[5,64,128]{2,1,0:T(8,128)(2,1)}, bf16[5,64,128]{2,1,0:T(8,128)(2,1)S(1)}, u32[]{:S(2)}, u32[]{:S(2)}) collective-permute-start(bf16[5,64,128]{2,1,0:T(8,128)(2,1)} %get-tuple-element.39), channel_id=1, source_target_pairs={{0,8},{8,16},{16,24},{1,9},{9,17},{17,25},{2,10},{10,18},{18,26},{... | collective-permute-start | bytes 245768 | tf_op jit(solution)/shard_map/ppermute | solution.py:478
  111.7 6.0 %collective-permute-start.7 = (bf16[5,64,128]{2,1,0:T(8,128)(2,1)}, bf16[5,64,128]{2,1,0:T(8,128)(2,1)S(1)}, u32[]{:S(2)}, u32[]{:S(2)}) collective-permute-start(bf16[5,64,128]{2,1,0:T(8,128)(2,1)} %get-tuple-element.40), channel_id=1, source_target_pairs={{8,0},{16,8},{24,16},{9,1},{17,9},{25,17},{10,2},{18,10},{26,18},{... | collective-permute-start | bytes 245768 | tf_op jit(solution)/shard_map/ppermute | solution.py:478
  113.7 4.0 %copy-start.3 = (bf16[5,64,128]{2,1,0:T(8,128)(2,1)}, bf16[5,64,128]{2,1,0:T(8,128)(2,1)S(1)}, u32[]{:S(2)}) copy-start(bf16[5,64,128]{2,1,0:T(8,128)(2,1)S(1)} %collective-permute-done.6.top_ref.top_edge_ref) | copy-start | bytes 245764
  (6 other events, 3.8 us)

commit v2 on v0

v2 whole, which is shorter than its diff:
```python
import functools
import math

import jax
import jax.numpy as jnp
from jax import lax
from jax.experimental import pallas as pl
from jax.experimental.pallas import tpu as pltpu
from jax.sharding import PartitionSpec as P


DILATION = 8
LANES = 128
LABEL_ROWS = 16
CHUNK = 16
F32 = jnp.float32
BF16 = jnp.bfloat16
NT = (((1,), (1,)), ((), ()))
VMEM = pl.BlockSpec(memory_space=pltpu.VMEM)
HBM = pl.BlockSpec(memory_space=pltpu.HBM)
SMEM = pl.BlockSpec(memory_space=pltpu.SMEM)


def mm(left, right):
    return jnp.dot(left, right, preferred_element_type=F32)


def mm_back(left, right):
    return lax.dot_general(left, right, NT, preferred_element_type=F32)


def turn(value, shift):
    if isinstance(shift, int):
        shift = shift % LANES
        if shift == 0:
            return value
    return pltpu.roll(value, shift, 1)


def lane_index(shape):
    return lax.broadcasted_iota(jnp.int32, shape, len(shape) - 1)


def regroup(row_groups):
    cells = LANES // row_groups
    shape = (row_groups * LANES, 4 * LANES)
    raw = lax.broadcasted_iota(jnp.int32, shape, 0)
    grouped = lax.broadcasted_iota(jnp.int32, shape, 1)
    group, col = raw // LANES, raw % LANES
    place = (col % 4) * LANES + group * cells + col // 4
    return jnp.where(place == grouped, 1.0, 0.0).astype(BF16)


def row_windows(row, edge):
    lane = lane_index(row.shape)
    low = jnp.where(lane < DILATION, edge, turn(row, DILATION))
    high = jnp.where(lane >= LANES - DILATION, edge, turn(row, -DILATION))
    return (low, row, high)


class Framed:
    def __init__(self, body, low, high, top, bottom, step):
        self.rows = body.shape[1]
        self.refs = (body, low, high, top, bottom)
        self.step = step

    def windows(self, start, size):
        body, low, high, top, bottom = self.refs
        span = pl.ds(start, size)
        step = self.step
        edge_low = low[step, span, :].astype(F32)
        edge_high = turn(high[step, span, :].astype(F32), -DILATION)
        odd_slot = (lane_index(edge_low.shape) // DILATION) % 2 == 1
        edges = (
            jnp.where(odd_slot, edge_high, edge_low),
            jnp.where(odd_slot, edge_low, edge_high),
        )
        shift = (LANES - DILATION) - step * (2 * DILATION)
        for row in range(-1, self.rows + 1):
            if 0 <= row < self.rows:
                value = body[step, row, span, :].astype(F32)
                edge = turn(edges[row % 2], -DILATION * row)
            else:
                source = top if row < 0 else bottom
                value = source[step, span, :].astype(F32)
                edge = turn(source[source.shape[0] - 1, span, :].astype(F32), shift)
            yield row, row_windows(value, edge)


def depthwise_chunk(framed, start, size, taps, emit):
    sums = {}
    for row, windows in framed.windows(start, size):
        for above in range(3):
            target = row + 1 - above
            if not 0 <= target < framed.rows:
                continue
            for side in range(3):
                term = taps[3 * above + side] * windows[side]
                sums[target] = sums[target] + term if target in sums else term
        if row - 1 >= 0:
            emit(row - 1, sums.pop(row - 1))


def tap_columns(kernel_ref, start, size, flip):
    block = kernel_ref[pl.ds(start, size), :]
    order = [8 - tap if flip else tap for tap in range(9)]
    return [jnp.broadcast_to(block[:, tap : tap + 1], (size, LANES)) for tap in order]


def edge_columns(row_of, rows):
    low = high = None
    for row in range(rows):
        value = row_of(row)
        slot = lane_index(value.shape) // DILATION == row
        to_low = turn(value, DILATION * row)
        to_high = turn(value, DILATION * row + DILATION)
        low = jnp.where(slot, to_low, 0.0 if low is None else low)
        high = jnp.where(slot, to_high, 0.0 if high is None else high)
    return low.astype(BF16), high.astype(BF16)


def split_kernel(x_ref, rows_ref, low_ref, high_ref, flat):
    slices, channels, rows = x_ref.shape[:3]

    def one_slice(step, carry):
        flat[...] = x_ref[step].reshape(channels * rows, LANES).astype(F32)

        def row_of(row):
            value = flat[pl.ds(row, channels, stride=rows), :]
            rows_ref[step, row] = value.astype(BF16)
            return value

        low_ref[step], high_ref[step] = edge_columns(row_of, rows)
        return carry

    lax.fori_loop(0, slices, one_slice, 0)


def start_state(state_ref, kernel_ref, down_ref, table, start, taps_ref, down_back, flat, tap_rows):
    channels, rows = state_ref.shape[0], state_ref.shape[1]
    table[...] = regroup(rows // 4)
    flat[...] = state_ref[...].reshape(channels * rows, LANES).astype(F32)
    for phase in range(4):
        parts = [
            flat[pl.ds(row, channels, stride=rows), :].astype(BF16)
            for row in range(phase, rows, 4)
        ]
        start[phase * channels : (phase + 1) * channels, :] = mm(
            jnp.concatenate(parts, axis=1), table[...]
        )
    down_back[...] = down_ref[...].astype(F32).T.astype(BF16)
    tap_rows[...] = jnp.zeros_like(tap_rows)
    for above in range(3):
        tap_rows[3 * above : 3 * above + 3, :channels] = kernel_ref[above]
    taps_ref[...] = tap_rows[...].T[:channels]


def message_kernel(rows_ref, low_ref, high_ref, down_ref, up_ref):
    slices = rows_ref.shape[0]
    corner_down = corner_up = jnp.zeros(rows_ref.shape[2:], F32)
    for step in range(slices):
        down_ref[step] = rows_ref[step, rows_ref.shape[1] - 1]
        up_ref[step] = rows_ref[step, 0]
        base = 2 * DILATION * step
        low = low_ref[step].astype(F32)
        high = high_ref[step].astype(F32)
        slot = lane_index(low.shape) // DILATION
        corner_down = jnp.where(slot == 2 * step, turn(high, base + DILATION), corner_down)
        corner_down = jnp.where(
            slot == 2 * step + 1, turn(low, base + 2 * DILATION), corner_down
        )
        corner_up = jnp.where(slot == 2 * step, turn(high, base), corner_up)
        corner_up = jnp.where(slot == 2 * step + 1, turn(low, base + DILATION), corner_up)
    down_ref[slices] = corner_down.astype(BF16)
    up_ref[slices] = corner_up.astype(BF16)


def recur_kernel(
    ranks,
    scale,
    plan,
    x_ref,
    low_ref,
    high_ref,
    top_ref,
    bottom_ref,
    state_ref,
    kernel_ref,
    weight_ref,
    down_ref,
    *rest,
):
    cot_refs, rest = rest[:ranks], rest[ranks:]
    out_hbms, rest = rest[:ranks], rest[ranks:]
    rows_ref, edge_low_ref, edge_high_ref, grad_state_ref, packed_ref, taps_ref, *rest = rest
    keep, stack, state, conv, patch, down_sum, out_ref, dense, tap_sums, flat, *rest = rest
    table, down_back, tap_rows, cots, sems = rest
    start_state(
        state_ref, kernel_ref, down_ref, table, state, taps_ref, down_back, flat, tap_rows
    )
    for rank, cot_ref in enumerate(cot_refs):
        cots[rank] = cot_ref[...]
    slices, rows, channels = x_ref.shape[:3]
    blocks = x_ref.shape[0]
    down_sum[...] = jnp.zeros_like(down_sum)
    out_ref[:, :, LANES:, :] = jnp.zeros_like(out_ref[:, :, LANES:, :])
    size = CHUNK

    def slot_of(step):
        owner = jnp.clip(plan[step], 0, ranks - 1)
        return owner, jnp.clip(plan[blocks + step], 0, blocks - 1)

    def back_of(step):
        owner, dest = slot_of(step)
        return cots[jnp.bitwise_xor(owner, plan[2 * blocks]), dest]

    def forward_slice(step, outer):
        framed = Framed(x_ref, low_ref, high_ref, top_ref, bottom_ref, step)

        def conv_chunk(index, carry):
            start = pl.multiple_of(index * size, size)
            taps = tap_columns(taps_ref, start, size, False)

            def emit(row, value):
                conv[row, pl.ds(start, size), :] = value.astype(BF16)

            depthwise_chunk(framed, start, size, taps, emit)
            return carry

        lax.fori_loop(0, channels // size, conv_chunk, 0)
        wide = jnp.concatenate(
            [
                jnp.concatenate([conv[row] for row in range(phase, rows, 4)], axis=1)
                for phase in range(4)
            ],
            axis=0,
        )
        grouped = mm(wide, table[...]).astype(BF16)
        for phase in range(4):
            own = slice(phase * channels, (phase + 1) * channels)
            prior = state[own, :]
            stacked = jnp.concatenate([grouped[own], prior.astype(BF16)], axis=0)
            stack[step, phase] = stacked
            pre = mm(weight_ref[...], stacked)
            signed_update = jnp.tanh(0.5 * pre[:channels])
            signed_reset = jnp.tanh(0.5 * pre[channels : 2 * channels])
            update = 0.5 + 0.5 * signed_update
            stay = 0.5 - 0.5 * signed_update
            reset = 0.5 + 0.5 * signed_reset
            recurrent = pre[3 * channels :]
            candidate = jnp.tanh(pre[2 * channels : 3 * channels] + reset * recurrent)
            following = stay * prior + update * candidate
            state[own, :] = following
            act = update * (1.0 - candidate * candidate)
            act_reset = act * reset
            keep[step, 0, own, :] = (candidate - prior) * update * stay
            keep[step, 1, own, :] = act_reset * recurrent * (0.5 - 0.5 * signed_reset)
            keep[step, 2, own, :] = act
            keep[step, 3, own, :] = act_reset
            keep[step, 4, own, :] = stay
            rounded = following.astype(BF16).astype(F32)
            for col in range(4):
                patch[pl.ds(4 * phase + col, channels, stride=16), :] = rounded[
                    :, col * LANES : (col + 1) * LANES
                ]
        patched = patch[...].astype(BF16)
        owner, dest = slot_of(step)
        position = jnp.int32(0)
        for earlier in range(blocks):
            position += jnp.where((earlier < step) & (plan[earlier] == owner), 1, 0)
        position = jnp.minimum(position, out_ref.shape[1] - 1)
        distance = lax.rem(owner + ranks - plan[2 * blocks], ranks)
        block = mm(down_ref[...], patched).astype(BF16)
        label = (dest + 1).astype(F32)
        labels = jnp.full((LABEL_ROWS, LANES), label, F32).astype(BF16)
        out_ref[distance, position, :LANES, :] = block
        out_ref[distance, position, LANES:, :] = labels
        down_sum[...] += mm_back(back_of(step), patched)
        return outer

    lax.fori_loop(0, slices, forward_slice, 0)
    copies = [
        pltpu.make_async_copy(out_ref.at[rank], out_hbms[rank], sems.at[rank])
        for rank in range(ranks)
    ]
    for copy in copies:
        copy.start()
    carry = state
    carry[...] = jnp.zeros_like(carry)
    dense[...] = jnp.zeros_like(dense)
    tap_sums[...] = jnp.zeros_like(tap_sums)
    weight_back = weight_ref[...].astype(F32).T.astype(BF16)

    def backward_slice(index, outer):
        step = slices - 1 - index
        patch[...] = mm(down_back[...], back_of(step))
        flat_grads = []
        for phase in range(4):
            own = slice(phase * channels, (phase + 1) * channels)
            unpatched = jnp.concatenate(
                [patch[pl.ds(4 * phase + col, channels, stride=16), :] for col in range(4)],
                axis=1,
            )
            flow = carry[own, :] + unpatched
            delta = jnp.concatenate(
                [(flow * keep[step, part, own, :]).astype(BF16) for part in range(4)],
                axis=0,
            )
            reverse = mm(weight_back, delta)
            carry[own, :] = keep[step, 4, own, :] * flow + reverse[channels:]
            flat_grads.append(reverse[:channels].astype(BF16))
            dense[...] += lax.dot_general(
                delta, stack[step, phase], NT, preferred_element_type=F32
            )
        spread = mm_back(jnp.concatenate(flat_grads, axis=0), table[...])

        def row_of(row):
            group, phase = row // 4, row % 4
            value = spread[
                phase * channels : (phase + 1) * channels, group * LANES : (group + 1) * LANES
            ]
            rows_ref[step, row] = value.astype(BF16)
            return value

        edge_low_ref[step], edge_high_ref[step] = edge_columns(row_of, rows)
        framed = Framed(x_ref, low_ref, high_ref, top_ref, bottom_ref, step)

        def tap_chunk(index, loop_carry):
            start = pl.multiple_of(index * size, size)
            span = pl.ds(start, size)
            sums = [tap_sums[tap, span, :] for tap in range(9)]
            for row, windows in framed.windows(start, size):
                for above in range(3):
                    target = row + 1 - above
                    if not 0 <= target < rows:
                        continue
                    grad = rows_ref[step, target, span, :].astype(F32)
                    for side in range(3):
                        tap = 3 * above + side
                        sums[tap] = sums[tap] + grad * windows[side]
            for tap in range(9):
                tap_sums[tap, span, :] = sums[tap]
            return loop_carry

        lax.fori_loop(0, channels // size, tap_chunk, 0)
        return outer

    lax.fori_loop(0, slices, backward_slice, 0)
    remain = carry[...]
    total = None
    for _ in range(3):
        piece = remain.astype(BF16)
        remain = remain - piece.astype(F32)
        term = mm_back(piece, table[...])
        total = term if total is None else total + term
    for phase in range(4):
        for group in range(rows // 4):
            flat[pl.ds(4 * group + phase, channels, stride=rows), :] = total[
                phase * channels : (phase + 1) * channels,
                group * LANES : (group + 1) * LANES,
            ]
    grad_state_ref[...] = flat[...].reshape(channels, rows, LANES)
    lower = dense[2 * channels : 3 * channels, :]
    upper = dense[3 * channels :, :]
    merged = jnp.where(lane_index(lower.shape) < channels, lower, upper)
    gathered = jnp.zeros((channels, LANES), F32)
    for tap in range(9):
        column = jnp.sum(tap_sums[tap], axis=1, keepdims=True)
        gathered = jnp.where(lane_index(gathered.shape) == tap, column, gathered)
    tap_rows = jnp.concatenate(
        [gathered.T[:16], jnp.zeros((16, LANES - channels), F32)], axis=1
    )
    shares = packed_ref.shape[0]
    parts = [dense[: 2 * channels, :], merged, tap_rows]
    parts.append(jnp.zeros((8 * shares - 3 * channels - 16, LANES), F32))
    small = jnp.concatenate(parts, axis=0) * scale
    packed_ref[:, :16, :] = paired(small.reshape(shares, 8, LANES))
    for part in range(down_sum.shape[1] // LANES):
        value = down_sum[:, part * LANES : (part + 1) * LANES] * scale
        value = value.reshape((-1, packed_ref.shape[1] - 16, LANES))
        first = part * value.shape[0]
        packed_ref[first : first + value.shape[0], 16:, :] = value.astype(BF16)
    for copy in copies:
        copy.wait()


def paired(value):
    rounded = value.astype(BF16).astype(F32)
    return jnp.concatenate([rounded, value - rounded], axis=-2).astype(BF16)


def summed(pieces_ref):
    total = pieces_ref[0].astype(F32)
    for share in range(1, pieces_ref.shape[0]):
        total = total + pieces_ref[share].astype(F32)
    return total


def share_kernel(pieces_ref, out_ref):
    total = summed(pieces_ref)
    small = paired(total[:8] + total[8:16])
    down = total[16:].astype(BF16)
    for share in range(out_ref.shape[0]):
        out_ref[share, :16] = small
        out_ref[share, 16:] = down


def features_kernel(x_ref, low_ref, high_ref, top_ref, bottom_ref, taps_ref, out_ref, flat):
    slices, rows, channels = x_ref.shape[:3]
    size = CHUNK

    def one_slice(step, outer):
        framed = Framed(x_ref, low_ref, high_ref, top_ref, bottom_ref, step)

        def conv_chunk(index, carry):
            start = pl.multiple_of(index * size, size)
            taps = tap_columns(taps_ref, start, size, True)

            def emit(row, value):
                flat[pl.ds(start * rows + row, size, stride=rows), :] = value

            depthwise_chunk(framed, start, size, taps, emit)
            return carry

        lax.fori_loop(0, channels // size, conv_chunk, 0)
        out_ref[step] = flat[...].reshape(channels, rows, LANES).astype(BF16)
        return outer

    lax.fori_loop(0, slices, one_slice, 0)


def landing(arrived_refs, cart_ref):
    for dest in range(cart_ref.shape[0]):
        total = jnp.zeros(cart_ref.shape[1:], F32)
        for arrived_ref in arrived_refs:
            for slot in range(arrived_ref.shape[0]):
                label = arrived_ref[slot, LANES : LANES + LABEL_ROWS, :].astype(F32)[:1]
                value = arrived_ref[slot, :LANES, :].astype(F32)
                total = total + jnp.where(label == dest + 1, value, 0.0)
        cart_ref[dest] = total


def finish_kernel(spread_ref, *refs):
    *arrived_refs, gate_ref, cand_ref, recur_ref, taps_ref, down_ref, cart_ref = refs
    landing(arrived_refs, cart_ref)
    channels = cand_ref.shape[0]
    coarse_ch = down_ref.shape[0]
    shares = spread_ref.shape[0]
    small = spread_ref[:, :16, :].astype(F32)
    total = (small[:, :8] + small[:, 8:]).reshape(8 * shares, LANES)
    gate_ref[...] = total[: 2 * channels]
    cand_ref[...] = total[2 * channels : 3 * channels, :channels]
    recur_ref[...] = total[2 * channels : 3 * channels, channels:]
    for above in range(3):
        first = 3 * channels + 3 * above
        taps_ref[above] = total[first : first + 3, :channels]
    down = spread_ref[:, 16:, :].astype(F32).reshape(down_ref.shape[1] // LANES, coarse_ch, LANES)
    for part in range(down.shape[0]):
        down_ref[:, part * LANES : (part + 1) * LANES] = down[part]


def shifted(value, axis, distance, periodic):
    count = lax.axis_size(axis)
    pairs = [(i, i + 1) for i in range(count - 1)]
    if periodic:
        pairs.append((count - 1, 0))
    if distance < 0:
        pairs = [(target, source) for source, target in pairs]
    return lax.ppermute(value, axis, pairs)


def exchange(rows_array, edge_low, edge_high):
    slices, _, channels, _ = rows_array.shape
    low = shifted(edge_high, "azimuth", 1, True)
    high = shifted(edge_low, "azimuth", -1, True)
    message = jax.ShapeDtypeStruct((slices + 1, channels, LANES), BF16)
    down, up = pl.pallas_call(
        message_kernel,
        in_specs=[VMEM] * 3,
        out_specs=[VMEM] * 2,
        out_shape=[message] * 2,
        name="message",
        compiler_params=params(),
        cost_estimate=cost(1),
    )(rows_array, low, high)
    top = shifted(down, "range", 1, False)
    bottom = shifted(up, "range", -1, False)
    return (rows_array, low, high, top, bottom)


def params(mib=12):
    return pltpu.CompilerParams(vmem_limit_bytes=mib << 20)


def cost(mib, flops=1 << 20):
    return pl.CostEstimate(flops=flops, bytes_accessed=int(mib * (1 << 20)), transcendentals=0)


def on_device(
    features,
    state_init,
    kernel,
    gate_weight,
    cand_weight,
    recur_weight,
    down_weight,
    owner_map,
    dest_map,
    cart_cot,
):
    slices, channels, rows, cols = features.shape
    coarse_ch = down_weight.shape[0]
    ranks = lax.axis_size("range")
    shares = ranks * lax.axis_size("azimuth")
    blocks = owner_map.shape[2]
    capacity = blocks // 2
    assert cols == LANES and rows * DILATION == LANES and blocks == slices
    scale = 1.0 / math.sqrt(slices * rows * cols * shares)
    me = lax.axis_index("range").astype(jnp.int32)
    plan = jnp.concatenate(
        [owner_map.reshape(blocks), dest_map.reshape(blocks), me.reshape(1)]
    )
    empty = jnp.zeros(cand_weight.shape, BF16)
    weights = jnp.concatenate(
        [
            gate_weight,
            jnp.concatenate([cand_weight, empty], axis=1),
            jnp.concatenate([empty, recur_weight], axis=1),
        ],
        axis=0,
    )
    flat_scratch = pltpu.VMEM((channels * rows, LANES), F32)
    row_shape = jax.ShapeDtypeStruct((slices, rows, channels, LANES), BF16)
    edge_shape = jax.ShapeDtypeStruct((slices, channels, LANES), BF16)
    cot_shape = jax.ShapeDtypeStruct((blocks, coarse_ch, LANES), BF16)
    group = (4 * channels, 4 * LANES)
    out_blocks = jax.ShapeDtypeStruct((capacity, coarse_ch + LABEL_ROWS, LANES), BF16)
    down_rows = 16 * channels * coarse_ch // (LANES * shares)
    packed_shape = jax.ShapeDtypeStruct((shares, 16 + down_rows, LANES), BF16)
    everyone = ("range", "azimuth")

    pieces = {0: cart_cot.reshape(cot_shape.shape)}
    gap = ranks // 2
    far = lax.ppermute(pieces[0], "range", [(i, i ^ gap) for i in range(ranks)])
    arranged, edge_low, edge_high = pl.pallas_call(
        split_kernel,
        in_specs=[VMEM],
        out_specs=[VMEM] * 3,
        out_shape=[row_shape, edge_shape, edge_shape],
        scratch_shapes=[flat_scratch],
        name="split",
        compiler_params=params(),
        cost_estimate=cost(3),
    )(features)
    frame = exchange(arranged, edge_low, edge_high)
    pieces[gap] = far
    gap //= 2
    while gap:
        for rank in list(pieces):
            pieces[rank ^ gap] = lax.ppermute(
                pieces[rank], "range", [(i, i ^ gap) for i in range(ranks)]
            )
        gap //= 2
    *outgoing, rows_grad, low_grad, high_grad, grad_state, packed, taps = pl.pallas_call(
        functools.partial(recur_kernel, ranks, scale),
        in_specs=[SMEM] + [VMEM] * (9 + ranks),
        out_specs=[HBM] * ranks + [VMEM] * 6,
        out_shape=[out_blocks] * ranks
        + [
            row_shape,
            edge_shape,
            edge_shape,
            jax.ShapeDtypeStruct((channels, rows, LANES), F32),
            packed_shape,
            jax.ShapeDtypeStruct((channels, 16), F32),
        ],
        scratch_shapes=[
            pltpu.VMEM((slices, 5) + group, F32),
            pltpu.VMEM((slices, 4, 2 * channels, 4 * LANES), BF16),
            pltpu.VMEM(group, F32),
            pltpu.VMEM((rows, channels, LANES), BF16),
            pltpu.VMEM((16 * channels, LANES), F32),
            pltpu.VMEM(down_weight.shape, F32),
            pltpu.VMEM((ranks,) + out_blocks.shape, BF16),
            pltpu.VMEM((4 * channels, 2 * channels), F32),
            pltpu.VMEM((9, channels, LANES), F32),
            flat_scratch,
            pltpu.VMEM((rows // 4 * LANES, 4 * LANES), BF16),
            pltpu.VMEM(down_weight.shape[::-1], BF16),
            pltpu.VMEM((16, LANES), F32),
            pltpu.VMEM((ranks,) + cot_shape.shape, BF16),
            pltpu.SemaphoreType.DMA((ranks,)),
        ],
        name="recur",
        compiler_params=params(28),
        cost_estimate=cost(16, 1 << 31),
    )(
        plan,
        *frame,
        state_init,
        kernel.transpose(1, 2, 0),
        weights,
        down_weight,
        *[pieces[rank] for rank in range(ranks)],
    )

    pieces = lax.all_to_all(packed, everyone, 0, 0, tiled=True)
    frame_grad = exchange(rows_grad, low_grad, high_grad)
    arrived = [outgoing[0]] + [
        lax.ppermute(outgoing[rank], "range", [(i, (i + rank) % ranks) for i in range(ranks)])
        for rank in range(1, ranks)
    ]
    shared = pl.pallas_call(
        share_kernel,
        in_specs=[VMEM],
        out_specs=VMEM,
        out_shape=packed_shape,
        name="share",
        compiler_params=params(),
        cost_estimate=cost(1),
    )(pieces)
    spread = lax.all_to_all(shared, everyone, 0, 0, tiled=True)
    grad_features = pl.pallas_call(
        features_kernel,
        in_specs=[VMEM] * 6,
        out_specs=VMEM,
        out_shape=jax.ShapeDtypeStruct(features.shape, BF16),
        scratch_shapes=[flat_scratch],
        name="features",
        compiler_params=params(),
        cost_estimate=cost(4, 1 << 25),
    )(*frame_grad, taps)
    grad_gate, grad_cand, grad_recur, grad_taps, grad_down, cartesian = pl.pallas_call(
        finish_kernel,
        in_specs=[VMEM] * (1 + ranks),
        out_specs=[VMEM] * 6,
        out_shape=[
            jax.ShapeDtypeStruct(gate_weight.shape, F32),
            jax.ShapeDtypeStruct(cand_weight.shape, F32),
            jax.ShapeDtypeStruct(recur_weight.shape, F32),
            jax.ShapeDtypeStruct((3, 3, channels), F32),
            jax.ShapeDtypeStruct(down_weight.shape, F32),
            jax.ShapeDtypeStruct(cot_shape.shape, F32),
        ],
        name="finish",
        compiler_params=params(),
        cost_estimate=cost(1),
    )(spread, *arrived)
    return (
        cartesian.reshape(cart_cot.shape),
        grad_features,
        grad_state,
        grad_taps.transpose(2, 0, 1),
        grad_gate,
        grad_cand,
        grad_recur,
        grad_down,
    )


def solution(mesh):
    placed = (
        P(None, None, "range", "azimuth"),
        P(None, "range", "azimuth"),
        P(),
        P(),
        P(),
        P(),
        P(),
        P("range", "azimuth", None),
        P("range", "azimuth", None),
        P("range", "azimuth", None, None, None),
    )
    return jax.shard_map(
        on_device,
        mesh=mesh,
        in_specs=placed,
        out_specs=(
            P("range", "azimuth", None, None, None),
            P(None, None, "range", "azimuth"),
            P(None, "range", "azimuth"),
            P(),
            P(),
            P(),
            P(),
            P(),
        ),
        check_vma=False,
    )
```

time: 502 us -> 93.6 us (0.19); the launches traced: 494 us -> 93.3 us
  waiting for transfers between devices: 140 us -> 14.8 us
  local copies, waits for them, and re-layouts: 94.2 us -> 1.91 us
  starting transfers between devices: 95.3 us -> 28.2 us
  matrix products: 62.9 us -> 0 us
  other arithmetic: 46.4 us -> 0.16 us
  Pallas kernels: 0 us -> 30 us
  blocking collectives: 38 us -> 17.5 us
  between operations: 16.7 us -> 0.78 us
    ppermute x32 -> x14, waiting for transfers between devices: 82.3 us -> 14.8 us  [the longest x8 14.8 us: shifted(): return lax.ppermute(value, axis, pairs)]
    dot_general x52 -> x0, matrix products: 62.9 us -> none  [the longest x18 24.8 us: back_product(): lax.dot_general(weight, grads, (((0,), (0,)), ((), ())), preferred_elemen...]
    psum x1 -> x0, waiting for transfers between devices: 57.9 us -> none  [on_device(): lax.psum((grad_kernel, grad_gate, grad_cand, grad_recur, grad_down), ('ra...]
    ppermute x32 -> x14, starting transfers between devices: 82.9 us -> 25.2 us  [the longest x8 19.5 us: shifted(): return lax.ppermute(value, axis, pairs)]
    psum x1 -> x0, blocking collectives: 38 us -> none  [on_device(): lax.psum((grad_kernel, grad_gate, grad_cand, grad_recur, grad_down), ('ra...]
    reshape x15 -> x0, local copies, waits for them, and re-layouts: 32 us -> none  [the longest x4 11.6 us: unpatches(): grads.reshape(channels, 4, 4, tile_rows // 4, tile_cols // 4)]
    pallas_call x0 -> x7, Pallas kernels: none -> 30 us  [the longest x1 21.6 us: on_device(): pl.pallas_call(functools.partial(recur_kernel, ranks, scale), in_specs=[S...]
    transpose x8 -> x0, local copies, waits for them, and re-layouts: 25 us -> none  [the longest x4 13.9 us: patches(): values.reshape(channels, tile_rows // 4, 4, tile_cols // 4, 4)]
  transfers between devices with their start and end apart: 36 -> 15, of which waited for: 15 -> 4; matrix products, arithmetic and copies ran while one was open for 29% -> 0% of each run, Pallas kernels for 0% -> 7%
where the time goes in v2:
time: 93.6 us; the launch traced here: 93.3 us
  Pallas kernels  30 us (32%)
  starting transfers between devices  28.2 us (30%)
  blocking collectives  17.5 us (19%)
  waiting for transfers between devices  14.8 us (16%)
  local copies, waits for them, and re-layouts  1.91 us (2%)
    pallas_call x1, Pallas kernels, on_device(): pl.pallas_call(functools.partial(recur_kernel, ranks, scale), in_specs=[S...  21.6 us
    ppermute x8, starting transfers between devices, shifted(): return lax.ppermute(value, axis, pairs)  19.5 us
    all_to_all x1, blocking collectives, on_device(): pieces = lax.all_to_all(packed, everyone, 0, 0, tiled=True)  17.5 us
    ppermute x8, waiting for transfers between devices, shifted(): return lax.ppermute(value, axis, pairs)  14.8 us
    pallas_call x1, Pallas kernels, on_device(): pl.pallas_call(features_kernel, in_specs=[VMEM] * 6, out_specs=VMEM, out_...  5.09 us
    all_to_all x1, starting transfers between devices, on_device(): spread = lax.all_to_all(shared, everyone, 0, 0, tiled=True)  2.94 us
    ppermute x3, starting transfers between devices, on_device(): lax.ppermute(outgoing[rank], 'range', [(i, (i + rank) % ranks) for i in r...  2.26 us
    ppermute x1, starting transfers between devices, on_device(): far = lax.ppermute(pieces[0], 'range', [(i, i ^ gap) for i in range(ranks)])  2.09 us
  transfers between devices with their start and end apart: 15, of which 4 were waited for; matrix products, arithmetic and copies ran while one was open for 0% of the time, Pallas kernels for 7%

profile of v2, /device:TPU:1, one launch (start us, length us, event | category | flops | bytes accessed | tf_op | source)
XLA Modules:
  0.0 93.3 jit_solution(12062263416608939864)
XLA Ops:
  0.6 2.1 %collective-permute-start.5 = (bf16[4,128,128]{2,1,0:T(8,128)(2,1)}, bf16[4,128,128]{2,1,0:T(8,128)(2,1)S(1)}, u32[]{:S(2)}, u32[]{:S(2)}) collective-permute-start(bf16[4,128,128]{2,1,0:T(8,128)(2,1)} %bitcast.7), channel_id=1, source_target_pairs={{0,16},{8,24},{16,0},{24,8},{1,17},{9,25},{17,1},{25,9},{2,18},{10... | collective-permute-start | bytes 393224 | tf_op jit(solution)/shard_map/ppermute | solution.py:544
  2.7 1.0 %collective-permute-start.4 = (bf16[4,128,128]{2,1,0:T(8,128)(2,1)}, bf16[4,128,128]{2,1,0:T(8,128)(2,1)S(1)}, u32[]{:S(2)}, u32[]{:S(2)}) collective-permute-start(bf16[4,128,128]{2,1,0:T(8,128)(2,1)} %bitcast.8), channel_id=1, source_target_pairs={{0,8},{8,0},{16,24},{24,16},{1,9},{9,1},{17,25},{25,17},{2,10},{10... | collective-permute-start | bytes 393224 | tf_op jit(solution)/shard_map/ppermute | solution.py:560
  3.7 1.2 %copy-done = bf16[4,64,16,128]{3,2,1,0:T(8,128)(2,1)S(1)} copy-done((bf16[4,64,16,128]{3,2,1,0:T(8,128)(2,1)S(1)}, bf16[4,64,16,128]{3,2,1,0:T(8,128)(2,1)}, u32[]{:S(2)}) %copy-start) | copy-done | bytes 1048600
  4.9 1.1 %split.1 = (bf16[4,16,64,128]{3,2,1,0:T(8,128)(2,1)S(1)}, bf16[4,64,128]{2,1,0:T(8,128)(2,1)S(1)}, bf16[4,64,128]{2,1,0:T(8,128)(2,1)S(1)}) custom-call(bf16[4,64,16,128]{3,2,1,0:T(8,128)(2,1)S(1)} %copy-done), custom_call_target="tpu_custom_call" | custom-call | flops 1048576 | bytes 3145728 | tf_op jit(solution)/shard_map/split/pallas_call | solution.py:545
  6.0 1.3 %collective-permute-start = (bf16[4,64,128]{2,1,0:T(8,128)(2,1)S(1)}, bf16[4,64,128]{2,1,0:T(8,128)(2,1)S(1)}, u32[]{:S(2)}, u32[]{:S(2)}) collective-permute-start(bf16[4,64,128]{2,1,0:T(8,128)(2,1)S(1)} %get-tuple-element.32), channel_id=1, source_target_pairs={{0,1},{1,2},{2,3},{3,4},{4,5},{5,6},{6,7},{7,0},{8,9},{9,10},{10,1... | collective-permute-start | bytes 196616 | tf_op jit(solution)/shard_map/ppermute | solution.py:469
  7.3 3.1 %collective-permute-start.1 = (bf16[4,64,128]{2,1,0:T(8,128)(2,1)S(1)}, bf16[4,64,128]{2,1,0:T(8,128)(2,1)S(1)}, u32[]{:S(2)}, u32[]{:S(2)}) collective-permute-start(bf16[4,64,128]{2,1,0:T(8,128)(2,1)S(1)} %get-tuple-element.33), channel_id=1, source_target_pairs={{1,0},{2,1},{3,2},{4,3},{5,4},{6,5},{7,6},{0,7},{9,8},{10,9},{11,1... | collective-permute-start | bytes 196616 | tf_op jit(solution)/shard_map/ppermute | solution.py:469
  10.9 1.8 %collective-permute-done.low_ref = bf16[4,64,128]{2,1,0:T(8,128)(2,1)S(1)} collective-permute-done((bf16[4,64,128]{2,1,0:T(8,128)(2,1)S(1)}, bf16[4,64,128]{2,1,0:T(8,128)(2,1)S(1)}, u32[]{:S(2)}, u32[]{:S(2)}) %collective-permute-start) | collective-permute-done | bytes 65568 | tf_op jit(solution)/shard_map/ppermute | solution.py:469
  12.8 2.9 %collective-permute-start.2 = (bf16[5,64,128]{2,1,0:T(8,128)(2,1)S(1)}, bf16[5,64,128]{2,1,0:T(8,128)(2,1)S(1)}, u32[]{:S(2)}, u32[]{:S(2)}) collective-permute-start(bf16[5,64,128]{2,1,0:T(8,128)(2,1)S(1)} %get-tuple-element.34), channel_id=1, source_target_pairs={{0,8},{8,16},{16,24},{1,9},{9,17},{17,25},{2,10},{10,18},{18,26},{... | collective-permute-start | bytes 245768 | tf_op jit(solution)/shard_map/ppermute | solution.py:469
  15.7 1.9 %collective-permute-start.3 = (bf16[5,64,128]{2,1,0:T(8,128)(2,1)S(1)}, bf16[5,64,128]{2,1,0:T(8,128)(2,1)S(1)}, u32[]{:S(2)}, u32[]{:S(2)}) collective-permute-start(bf16[5,64,128]{2,1,0:T(8,128)(2,1)S(1)} %get-tuple-element.35), channel_id=1, source_target_pairs={{8,0},{16,8},{24,16},{9,1},{17,9},{25,17},{10,2},{18,10},{26,18},{... | collective-permute-start | bytes 245768 | tf_op jit(solution)/shard_map/ppermute | solution.py:469
  17.7 0.6 copy-done.8
  18.4 3.1 %collective-permute-done.3.bottom_ref = bf16[5,64,128]{2,1,0:T(8,128)(2,1)S(1)} collective-permute-done((bf16[5,64,128]{2,1,0:T(8,128)(2,1)S(1)}, bf16[5,64,128]{2,1,0:T(8,128)(2,1)S(1)}, u32[]{:S(2)}, u32[]{:S(2)}) %collective-permute-start.3) | collective-permute-done | bytes 81952 | tf_op jit(solution)/shard_map/ppermute | solution.py:469
  21.5 21.6 %recur.1 = (bf16[2,144,128]{2,1,0:T(8,128)(2,1)S(1)}, bf16[2,144,128]{2,1,0:T(8,128)(2,1)S(1)}, bf16[2,144,128]{2,1,0:T(8,128)(2,1)S(1)}, bf16[2,144,128]{2,1,0:...) custom-call(s32[9]{0:T(128)S(1)} %pad_add_fusion.plan, ...), custom_call_target="tpu_custom_call" | custom-call | flops 2147483648 | bytes 16777216 | tf_op jit(solution)/shard_map/recur/pallas_call | solution.py:564
  43.1 17.5 %all_to_all.10.pieces_ref = bf16[32,48,128]{2,1,0:T(8,128)(2,1)S(1)} all-to-all(bf16[32,48,128]{2,1,0:T(8,128)(2,1)S(1)} %get-tuple-element.36), channel_id=1, replica_groups=mesh['range'=4,'azimuth'=8] {'range','azimuth'}, dimensions={0} | all-to-all | bytes 786432 | tf_op jit(solution)/shard_map/all_to_all | solution.py:607
  60.6 0.8 share.1
  61.4 2.9 %all-to-all-start.1 = ((bf16[32,48,128]{2,1,0:T(8,128)(2,1)}), bf16[32,48,128]{2,1,0:T(8,128)(2,1)S(1)}, u32[]{:S(2)}, u32[]{:S(2)}) async-start(bf16[32,48,128]{2,1,0:T(8,128)(2,1)} %share.1), calls=%async_computation.1 | async-start | bytes 786432 | tf_op jit(solution)/shard_map/all_to_all | solution.py:622
  64.4 1.4 %collective-permute-start.10 = (bf16[4,64,128]{2,1,0:T(8,128)(2,1)S(1)}, bf16[4,64,128]{2,1,0:T(8,128)(2,1)S(1)}, u32[]{:S(2)}, u32[]{:S(2)}) collective-permute-start(bf16[4,64,128]{2,1,0:T(8,128)(2,1)S(1)} %get-tuple-element.43), channel_id=1, source_target_pairs={{0,1},{1,2},{2,3},{3,4},{4,5},{5,6},{6,7},{7,0},{8,9},{9,10},{10,1... | collective-permute-start | bytes 196616 | tf_op jit(solution)/shard_map/ppermute | solution.py:469
  65.8 3.0 %collective-permute-start.11 = (bf16[4,64,128]{2,1,0:T(8,128)(2,1)S(1)}, bf16[4,64,128]{2,1,0:T(8,128)(2,1)S(1)}, u32[]{:S(2)}, u32[]{:S(2)}) collective-permute-start(bf16[4,64,128]{2,1,0:T(8,128)(2,1)S(1)} %get-tuple-element.44), channel_id=1, source_target_pairs={{1,0},{2,1},{3,2},{4,3},{5,4},{6,5},{7,6},{0,7},{9,8},{10,9},{11,1... | collective-permute-start | bytes 196616 | tf_op jit(solution)/shard_map/ppermute | solution.py:469
  68.8 8.4 %collective-permute-done.10.low_ref = bf16[4,64,128]{2,1,0:T(8,128)(2,1)S(1)} collective-permute-done((bf16[4,64,128]{2,1,0:T(8,128)(2,1)S(1)}, bf16[4,64,128]{2,1,0:T(8,128)(2,1)S(1)}, u32[]{:S(2)}, u32[]{:S(2)}) %collective-permute-start.10) | collective-permute-done | bytes 65568 | tf_op jit(solution)/shard_map/ppermute | solution.py:469
  77.3 4.0 %collective-permute-start.12 = (bf16[5,64,128]{2,1,0:T(8,128)(2,1)S(1)}, bf16[5,64,128]{2,1,0:T(8,128)(2,1)S(1)}, u32[]{:S(2)}, u32[]{:S(2)}) collective-permute-start(bf16[5,64,128]{2,1,0:T(8,128)(2,1)S(1)} %get-tuple-element.45), channel_id=1, source_target_pairs={{0,8},{8,16},{16,24},{1,9},{9,17},{17,25},{2,10},{10,18},{18,26},{... | collective-permute-start | bytes 245768 | tf_op jit(solution)/shard_map/ppermute | solution.py:469
  81.3 1.9 %collective-permute-start.13 = (bf16[5,64,128]{2,1,0:T(8,128)(2,1)S(1)}, bf16[5,64,128]{2,1,0:T(8,128)(2,1)S(1)}, u32[]{:S(2)}, u32[]{:S(2)}) collective-permute-start(bf16[5,64,128]{2,1,0:T(8,128)(2,1)S(1)} %get-tuple-element.46), channel_id=1, source_target_pairs={{8,0},{16,8},{24,16},{9,1},{17,9},{25,17},{10,2},{18,10},{26,18},{... | collective-permute-start | bytes 245768 | tf_op jit(solution)/shard_map/ppermute | solution.py:469
  83.2 1.8 %collective-permute-start.7 = (bf16[2,144,128]{2,1,0:T(8,128)(2,1)S(1)}, bf16[2,144,128]{2,1,0:T(8,128)(2,1)S(1)}, u32[]{:S(2)}, u32[]{:S(2)}) collective-permute-start(bf16[2,144,128]{2,1,0:T(8,128)(2,1)S(1)} %get-tuple-element.38), channel_id=1, source_target_pairs={{0,8},{8,16},{16,24},{24,0},{1,9},{9,17},{17,25},{25,1},{2,10},{10... | collective-permute-start | bytes 221192 | tf_op jit(solution)/shard_map/ppermute | solution.py:610
  85.5 1.6 %collective-permute-done.13.bottom_ref = bf16[5,64,128]{2,1,0:T(8,128)(2,1)S(1)} collective-permute-done((bf16[5,64,128]{2,1,0:T(8,128)(2,1)S(1)}, bf16[5,64,128]{2,1,0:T(8,128)(2,1)S(1)}, u32[]{:S(2)}, u32[]{:S(2)}) %collective-permute-start.13) | collective-permute-done | bytes 81952 | tf_op jit(solution)/shard_map/ppermute | solution.py:469
  87.0 5.1 %features.1 = bf16[4,64,16,128]{3,2,1,0:T(8,128)(2,1)} custom-call(bf16[4,16,64,128]{3,2,1,0:T(8,128)(2,1)S(1)} %get-tuple-element.42.rows_ref.x_ref, bf16[4,64,128]{2,1,0:T(8,128)(2,1)S(1)} %collective-permute-done.10.low_ref, bf16[4,64,128]{2,1,0:T(8,128)(2,1)S(1)} %collective-permute-done.11.high_ref, ...), custom_call_target="tpu_custom_call" | custom-call | flops 33554432 | bytes 4194304 | tf_op jit(solution)/shard_map/features/pallas_call | solution.py:623
  92.1 1.1 %finish.1 = (f32[128,128]{1,0:T(8,128)}, f32[64,64]{1,0:T(8,128)}, f32[64,64]{1,0:T(8,128)}, f32[3,3,64]{2,1,0:T(4,128)}, f32[128,1024]{1,0:T(8,128)}, /*index=5*/f32[4,128,128]{2,1,0:T(8,128)}) custom-call(bf16[32,48,128]{2,1,0:T(8,128)(2,1)S(1)} %all-to-all-done.1.spread_ref, bf16[2,144,128]{2,1,0:T(8,128)(2,1)S(1)} %get-tuple-element.37.refs_0_, ...), custom_call_target="tpu_custom_call" | custom-call | flops 1048576 | bytes 1048576 | tf_op jit(solution)/shard_map/finish/pallas_call | solution.py:633
  (36 shorter events, 1.4 us)
Async XLA Ops:
  0.6 9.8 %collective-permute-start.5 = (bf16[4,128,128]{2,1,0:T(8,128)(2,1)}, bf16[4,128,128]{2,1,0:T(8,128)(2,1)S(1)}, u32[]{:S(2)}, u32[]{:S(2)}) collective-permute-start(bf16[4,128,128]{2,1,0:T(8,128)(2,1)} %bitcast.7), channel_id=1, source_target_pairs={{0,16},{8,24},{16,0},{24,8},{1,17},{9,25},{17,1},{25,9},{2,18},{10... | collective-permute-start | bytes 393224 | tf_op jit(solution)/shard_map/ppermute | solution.py:544
  2.7 15.7 %collective-permute-start.4 = (bf16[4,128,128]{2,1,0:T(8,128)(2,1)}, bf16[4,128,128]{2,1,0:T(8,128)(2,1)S(1)}, u32[]{:S(2)}, u32[]{:S(2)}) collective-permute-start(bf16[4,128,128]{2,1,0:T(8,128)(2,1)} %bitcast.8), channel_id=1, source_target_pairs={{0,8},{8,0},{16,24},{24,16},{1,9},{9,1},{17,25},{25,17},{2,10},{10... | collective-permute-start | bytes 393224 | tf_op jit(solution)/shard_map/ppermute | solution.py:560
  3.7 1.2 %copy-start = (bf16[4,64,16,128]{3,2,1,0:T(8,128)(2,1)S(1)}, bf16[4,64,16,128]{3,2,1,0:T(8,128)(2,1)}, u32[]{:S(2)}) copy-start(bf16[4,64,16,128]{3,2,1,0:T(8,128)(2,1)} %x_ref.1) | copy-start | bytes 3145732
  4.9 5.9 %copy-start.5 = (bf16[128,128]{1,0:T(8,128)(2,1)S(1)}, bf16[128,128]{1,0:T(8,128)(2,1)}, u32[]{:S(2)}) copy-start(bf16[128,128]{1,0:T(8,128)(2,1)} %param.13) | copy-start | bytes 98308
  4.9 5.9 %copy-start.6 = (bf16[64,64]{1,0:T(8,128)(2,1)S(1)}, bf16[64,64]{1,0:T(8,128)(2,1)}, u32[]{:S(2)}) copy-start(bf16[64,64]{1,0:T(8,128)(2,1)} %param.15) | copy-start | bytes 24580
  4.9 5.9 %copy-start.7 = (bf16[64,64]{1,0:T(8,128)(2,1)S(1)}, bf16[64,64]{1,0:T(8,128)(2,1)}, u32[]{:S(2)}) copy-start(bf16[64,64]{1,0:T(8,128)(2,1)} %param.14) | copy-start | bytes 24580
  6.0 6.6 %collective-permute-start = (bf16[4,64,128]{2,1,0:T(8,128)(2,1)S(1)}, bf16[4,64,128]{2,1,0:T(8,128)(2,1)S(1)}, u32[]{:S(2)}, u32[]{:S(2)}) collective-permute-start(bf16[4,64,128]{2,1,0:T(8,128)(2,1)S(1)} %get-tuple-element.32), channel_id=1, source_target_pairs={{0,1},{1,2},{2,3},{3,4},{4,5},{5,6},{6,7},{7,0},{8,9},{9,10},{10,1... | collective-permute-start | bytes 196616 | tf_op jit(solution)/shard_map/ppermute | solution.py:469
  7.3 5.3 %collective-permute-start.1 = (bf16[4,64,128]{2,1,0:T(8,128)(2,1)S(1)}, bf16[4,64,128]{2,1,0:T(8,128)(2,1)S(1)}, u32[]{:S(2)}, u32[]{:S(2)}) collective-permute-start(bf16[4,64,128]{2,1,0:T(8,128)(2,1)S(1)} %get-tuple-element.33), channel_id=1, source_target_pairs={{1,0},{2,1},{3,2},{4,3},{5,4},{6,5},{7,6},{0,7},{9,8},{10,9},{11,1... | collective-permute-start | bytes 196616 | tf_op jit(solution)/shard_map/ppermute | solution.py:469
  10.4 11.1 %collective-permute-start.6 = (bf16[4,128,128]{2,1,0:T(8,128)(2,1)S(1)}, bf16[4,128,128]{2,1,0:T(8,128)(2,1)S(1)}, u32[]{:S(2)}, u32[]{:S(2)}) collective-permute-start(bf16[4,128,128]{2,1,0:T(8,128)(2,1)S(1)} %collective-permute-done.5.rest_2_), channel_id=1, source_target_pairs={{0,8},{8,0},{16,24},{24,16},{1,9},{9,1},{17,25},{25,17},{2,10},{10... | collective-permute-start | bytes 393224 | tf_op jit(solution)/shard_map/ppermute | solution.py:560
  12.7 8.9 %copy-start.1 = (bf16[64,16,128]{2,1,0:T(8,128)(2,1)S(1)}, bf16[64,16,128]{2,1,0:T(8,128)(2,1)}, u32[]{:S(2)}) copy-start(bf16[64,16,128]{2,1,0:T(8,128)(2,1)} %state_ref.1) | copy-start | bytes 786436
  12.7 8.9 %copy-start.2 = (bf16[128,1024]{1,0:T(8,128)(2,1)S(1)}, bf16[128,1024]{1,0:T(8,128)(2,1)}, u32[]{:S(2)}) copy-start(bf16[128,1024]{1,0:T(8,128)(2,1)} %down_ref.1) | copy-start | bytes 786436
  12.7 8.9 %copy-start.3 = (bf16[1,1,4,128,128]{4,3,2,1,0:T(8,128)(2,1)S(1)}, bf16[1,1,4,128,128]{4,3,2,1,0:T(8,128)(2,1)}, u32[]{:S(2)}) copy-start(bf16[1,1,4,128,128]{4,3,2,1,0:T(8,128)(2,1)} %param.19) | copy-start | bytes 393220
  12.8 8.7 %copy-start.4 = (f32[64,3,3]{0,2,1:T(4,128)S(1)}, f32[64,3,3]{0,2,1:T(4,128)}, u32[]{:S(2)}) copy-start(f32[64,3,3]{0,2,1:T(4,128)} %param.12) | copy-start | bytes 6916
  12.8 5.6 %collective-permute-start.2 = (bf16[5,64,128]{2,1,0:T(8,128)(2,1)S(1)}, bf16[5,64,128]{2,1,0:T(8,128)(2,1)S(1)}, u32[]{:S(2)}, u32[]{:S(2)}) collective-permute-start(bf16[5,64,128]{2,1,0:T(8,128)(2,1)S(1)} %get-tuple-element.34), channel_id=1, source_target_pairs={{0,8},{8,16},{16,24},{1,9},{9,17},{17,25},{2,10},{10,18},{18,26},{... | collective-permute-start | bytes 245768 | tf_op jit(solution)/shard_map/ppermute | solution.py:469
  15.7 5.8 %collective-permute-start.3 = (bf16[5,64,128]{2,1,0:T(8,128)(2,1)S(1)}, bf16[5,64,128]{2,1,0:T(8,128)(2,1)S(1)}, u32[]{:S(2)}, u32[]{:S(2)}) collective-permute-start(bf16[5,64,128]{2,1,0:T(8,128)(2,1)S(1)} %get-tuple-element.35), channel_id=1, source_target_pairs={{8,0},{16,8},{24,16},{9,1},{17,9},{25,17},{10,2},{18,10},{26,18},{... | collective-permute-start | bytes 245768 | tf_op jit(solution)/shard_map/ppermute | solution.py:469
  17.7 0.7 copy-start.9
  61.4 30.7 %all-to-all-start.1 = ((bf16[32,48,128]{2,1,0:T(8,128)(2,1)}), bf16[32,48,128]{2,1,0:T(8,128)(2,1)S(1)}, u32[]{:S(2)}, u32[]{:S(2)}) async-start(bf16[32,48,128]{2,1,0:T(8,128)(2,1)} %share.1), calls=%async_computation.1 | async-start | bytes 786432 | tf_op jit(solution)/shard_map/all_to_all | solution.py:622
  64.4 12.8 %collective-permute-start.10 = (bf16[4,64,128]{2,1,0:T(8,128)(2,1)S(1)}, bf16[4,64,128]{2,1,0:T(8,128)(2,1)S(1)}, u32[]{:S(2)}, u32[]{:S(2)}) collective-permute-start(bf16[4,64,128]{2,1,0:T(8,128)(2,1)S(1)} %get-tuple-element.43), channel_id=1, source_target_pairs={{0,1},{1,2},{2,3},{3,4},{4,5},{5,6},{6,7},{7,0},{8,9},{9,10},{10,1... | collective-permute-start | bytes 196616 | tf_op jit(solution)/shard_map/ppermute | solution.py:469
  65.8 11.3 %collective-permute-start.11 = (bf16[4,64,128]{2,1,0:T(8,128)(2,1)S(1)}, bf16[4,64,128]{2,1,0:T(8,128)(2,1)S(1)}, u32[]{:S(2)}, u32[]{:S(2)}) collective-permute-start(bf16[4,64,128]{2,1,0:T(8,128)(2,1)S(1)} %get-tuple-element.44), channel_id=1, source_target_pairs={{1,0},{2,1},{3,2},{4,3},{5,4},{6,5},{7,6},{0,7},{9,8},{10,9},{11,1... | collective-permute-start | bytes 196616 | tf_op jit(solution)/shard_map/ppermute | solution.py:469
  77.3 8.2 %collective-permute-start.12 = (bf16[5,64,128]{2,1,0:T(8,128)(2,1)S(1)}, bf16[5,64,128]{2,1,0:T(8,128)(2,1)S(1)}, u32[]{:S(2)}, u32[]{:S(2)}) collective-permute-start(bf16[5,64,128]{2,1,0:T(8,128)(2,1)S(1)} %get-tuple-element.45), channel_id=1, source_target_pairs={{0,8},{8,16},{16,24},{1,9},{9,17},{17,25},{2,10},{10,18},{18,26},{... | collective-permute-start | bytes 245768 | tf_op jit(solution)/shard_map/ppermute | solution.py:469
  81.3 5.8 %collective-permute-start.13 = (bf16[5,64,128]{2,1,0:T(8,128)(2,1)S(1)}, bf16[5,64,128]{2,1,0:T(8,128)(2,1)S(1)}, u32[]{:S(2)}, u32[]{:S(2)}) collective-permute-start(bf16[5,64,128]{2,1,0:T(8,128)(2,1)S(1)} %get-tuple-element.46), channel_id=1, source_target_pairs={{8,0},{16,8},{24,16},{9,1},{17,9},{25,17},{10,2},{18,10},{26,18},{... | collective-permute-start | bytes 245768 | tf_op jit(solution)/shard_map/ppermute | solution.py:469
  83.2 8.9 %collective-permute-start.7 = (bf16[2,144,128]{2,1,0:T(8,128)(2,1)S(1)}, bf16[2,144,128]{2,1,0:T(8,128)(2,1)S(1)}, u32[]{:S(2)}, u32[]{:S(2)}) collective-permute-start(bf16[2,144,128]{2,1,0:T(8,128)(2,1)S(1)} %get-tuple-element.38), channel_id=1, source_target_pairs={{0,8},{8,16},{16,24},{24,0},{1,9},{9,17},{17,25},{25,1},{2,10},{10... | collective-permute-start | bytes 221192 | tf_op jit(solution)/shard_map/ppermute | solution.py:610
  85.0 7.1 %collective-permute-start.8 = (bf16[2,144,128]{2,1,0:T(8,128)(2,1)S(1)}, bf16[2,144,128]{2,1,0:T(8,128)(2,1)S(1)}, u32[]{:S(2)}, u32[]{:S(2)}) collective-permute-start(bf16[2,144,128]{2,1,0:T(8,128)(2,1)S(1)} %get-tuple-element.39), channel_id=1, source_target_pairs={{0,16},{8,24},{16,0},{24,8},{1,17},{9,25},{17,1},{25,9},{2,18},{10... | collective-permute-start | bytes 221192 | tf_op jit(solution)/shard_map/ppermute | solution.py:610
  85.0 7.1 %collective-permute-start.9 = (bf16[2,144,128]{2,1,0:T(8,128)(2,1)S(1)}, bf16[2,144,128]{2,1,0:T(8,128)(2,1)S(1)}, u32[]{:S(2)}, u32[]{:S(2)}) collective-permute-start(bf16[2,144,128]{2,1,0:T(8,128)(2,1)S(1)} %get-tuple-element.40), channel_id=1, source_target_pairs={{0,24},{8,0},{16,8},{24,16},{1,25},{9,1},{17,9},{25,17},{2,26},{10... | collective-permute-start | bytes 221192 | tf_op jit(solution)/shard_map/ppermute | solution.py:610
  (1 other events, 0.7 us)

commit v3 on v2

--- a/solution.py
+++ b/solution.py
@@ -87,9 +87,11 @@
             yield row, row_windows(value, edge)
 
 
-def depthwise_chunk(framed, start, size, taps, emit):
+def depthwise_chunk(framed, start, size, taps, emit, save=None):
     sums = {}
     for row, windows in framed.windows(start, size):
+        if save is not None:
+            save(row, windows)
         for above in range(3):
             target = row + 1 - above
             if not 0 <= target < framed.rows:
@@ -194,7 +196,7 @@
     out_hbms, rest = rest[:ranks], rest[ranks:]
     rows_ref, edge_low_ref, edge_high_ref, grad_state_ref, packed_ref, taps_ref, *rest = rest
     keep, stack, state, conv, patch, down_sum, out_ref, dense, tap_sums, flat, *rest = rest
-    table, down_back, tap_rows, cots, sems = rest
+    table, down_back, tap_rows, cots, seen, wide_grad, sems = rest
     start_state(
         state_ref, kernel_ref, down_ref, table, state, taps_ref, down_back, flat, tap_rows
     )
@@ -205,6 +207,9 @@
     down_sum[...] = jnp.zeros_like(down_sum)
     out_ref[:, :, LANES:, :] = jnp.zeros_like(out_ref[:, :, LANES:, :])
     size = CHUNK
+    gate_rows = lax.broadcasted_iota(jnp.int32, weight_ref.shape, 0) < 2 * channels
+    weight = weight_ref[...].astype(F32)
+    half_weight = jnp.where(gate_rows, 0.5 * weight, weight).astype(BF16)
 
     def slot_of(step):
         owner = jnp.clip(plan[step], 0, ranks - 1)
@@ -224,7 +229,13 @@
             def emit(row, value):
                 conv[row, pl.ds(start, size), :] = value.astype(BF16)
 
-            depthwise_chunk(framed, start, size, taps, emit)
+            def save(row, windows):
+                lanes = slice((row + 1) * LANES, (row + 2) * LANES)
+                for side in range(3):
+                    span = pl.ds(side * channels + start, size)
+                    seen[step, span, lanes] = windows[side].astype(BF16)
+
+            depthwise_chunk(framed, start, size, taps, emit, save)
             return carry
 
         lax.fori_loop(0, channels // size, conv_chunk, 0)
@@ -237,32 +248,31 @@
         )
         grouped = mm(wide, table[...]).astype(BF16)
         for phase in range(4):
+            stack[step, phase, :channels, :] = grouped[phase * channels : (phase + 1) * channels]
+        for phase in range(4):
             own = slice(phase * channels, (phase + 1) * channels)
-            prior = state[own, :]
-            stacked = jnp.concatenate([grouped[own], prior.astype(BF16)], axis=0)
-            stack[step, phase] = stacked
-            pre = mm(weight_ref[...], stacked)
-            signed_update = jnp.tanh(0.5 * pre[:channels])
-            signed_reset = jnp.tanh(0.5 * pre[channels : 2 * channels])
-            update = 0.5 + 0.5 * signed_update
-            stay = 0.5 - 0.5 * signed_update
-            reset = 0.5 + 0.5 * signed_reset
-            recurrent = pre[3 * channels :]
-            candidate = jnp.tanh(pre[2 * channels : 3 * channels] + reset * recurrent)
-            following = stay * prior + update * candidate
-            state[own, :] = following
-            act = update * (1.0 - candidate * candidate)
-            act_reset = act * reset
-            keep[step, 0, own, :] = (candidate - prior) * update * stay
-            keep[step, 1, own, :] = act_reset * recurrent * (0.5 - 0.5 * signed_reset)
-            keep[step, 2, own, :] = act
-            keep[step, 3, own, :] = act_reset
-            keep[step, 4, own, :] = stay
-            rounded = following.astype(BF16).astype(F32)
             for col in range(4):
-                patch[pl.ds(4 * phase + col, channels, stride=16), :] = rounded[
-                    :, col * LANES : (col + 1) * LANES
-                ]
+                part = slice(col * LANES, (col + 1) * LANES)
+                prior = state[own, part]
+                stack[step, phase, channels:, part] = prior.astype(BF16)
+                pre = mm(half_weight, stack[step, phase, :, part])
+                half_update = 0.5 * jnp.tanh(pre[:channels])
+                half_reset = 0.5 * jnp.tanh(pre[channels : 2 * channels])
+                update = 0.5 + half_update
+                stay = 0.5 - half_update
+                reset = 0.5 + half_reset
+                recurrent = reset * pre[3 * channels :]
+                candidate = jnp.tanh(pre[2 * channels : 3 * channels] + recurrent)
+                step_by = update * (candidate - prior)
+                following = prior + step_by
+                state[own, part] = following
+                patch[pl.ds(4 * phase + col, channels, stride=16), :] = following
+                act = update * (1.0 - candidate * candidate)
+                keep[step, 0, own, part] = step_by * stay
+                keep[step, 1, own, part] = act * recurrent * (0.5 - half_reset)
+                keep[step, 2, own, part] = act
+                keep[step, 3, own, part] = act * reset
+                keep[step, 4, own, part] = stay
         patched = patch[...].astype(BF16)
         owner, dest = slot_of(step)
         position = jnp.int32(0)
@@ -319,30 +329,15 @@
             value = spread[
                 phase * channels : (phase + 1) * channels, group * LANES : (group + 1) * LANES
             ]
-            rows_ref[step, row] = value.astype(BF16)
+            rounded = value.astype(BF16)
+            rows_ref[step, row] = rounded
+            wide_grad[:, row * LANES : (row + 1) * LANES] = rounded
             return value
 
         edge_low_ref[step], edge_high_ref[step] = edge_columns(row_of, rows)
-        framed = Framed(x_ref, low_ref, high_ref, top_ref, bottom_ref, step)
-
-        def tap_chunk(index, loop_carry):
-            start = pl.multiple_of(index * size, size)
-            span = pl.ds(start, size)
-            sums = [tap_sums[tap, span, :] for tap in range(9)]
-            for row, windows in framed.windows(start, size):
-                for above in range(3):
-                    target = row + 1 - above
-                    if not 0 <= target < rows:
-                        continue
-                    grad = rows_ref[step, target, span, :].astype(F32)
-                    for side in range(3):
-                        tap = 3 * above + side
-                        sums[tap] = sums[tap] + grad * windows[side]
-            for tap in range(9):
-                tap_sums[tap, span, :] = sums[tap]
-            return loop_carry
-
-        lax.fori_loop(0, channels // size, tap_chunk, 0)
+        for above in range(3):
+            lanes = slice(above * LANES, (above + rows) * LANES)
+            tap_sums[above] += mm_back(wide_grad[...], seen[step, :, lanes])
         return outer
 
     lax.fori_loop(0, slices, backward_slice, 0)
@@ -365,7 +360,11 @@
     merged = jnp.where(lane_index(lower.shape) < channels, lower, upper)
     gathered = jnp.zeros((channels, LANES), F32)
     for tap in range(9):
-        column = jnp.sum(tap_sums[tap], axis=1, keepdims=True)
+        above, side = tap // 3, tap % 3
+        block = tap_sums[above]
+        own = lax.broadcasted_iota(jnp.int32, block.shape, 0) + side * channels
+        same = own == lane_index(block.shape)
+        column = jnp.sum(jnp.where(same, block, 0.0), axis=1, keepdims=True)
         gathered = jnp.where(lane_index(gathered.shape) == tap, column, gathered)
     tap_rows = jnp.concatenate(
         [gathered.T[:16], jnp.zeros((16, LANES - channels), F32)], axis=1
@@ -374,35 +373,24 @@
     parts = [dense[: 2 * channels, :], merged, tap_rows]
     parts.append(jnp.zeros((8 * shares - 3 * channels - 16, LANES), F32))
     small = jnp.concatenate(parts, axis=0) * scale
-    packed_ref[:, :16, :] = paired(small.reshape(shares, 8, LANES))
+    down_rows = packed_ref.shape[1] - 8
+    packed_ref[:, down_rows:, :] = small.reshape(shares, 8, LANES).astype(BF16)
     for part in range(down_sum.shape[1] // LANES):
         value = down_sum[:, part * LANES : (part + 1) * LANES] * scale
-        value = value.reshape((-1, packed_ref.shape[1] - 16, LANES))
+        value = value.reshape((-1, down_rows, LANES))
         first = part * value.shape[0]
-        packed_ref[first : first + value.shape[0], 16:, :] = value.astype(BF16)
+        packed_ref[first : first + value.shape[0], :down_rows, :] = value.astype(BF16)
     for copy in copies:
         copy.wait()
 
 
-def paired(value):
-    rounded = value.astype(BF16).astype(F32)
-    return jnp.concatenate([rounded, value - rounded], axis=-2).astype(BF16)
-
-
-def summed(pieces_ref):
+def share_kernel(pieces_ref, out_ref):
     total = pieces_ref[0].astype(F32)
     for share in range(1, pieces_ref.shape[0]):
         total = total + pieces_ref[share].astype(F32)
-    return total
-
-
-def share_kernel(pieces_ref, out_ref):
-    total = summed(pieces_ref)
-    small = paired(total[:8] + total[8:16])
-    down = total[16:].astype(BF16)
+    total = total.astype(BF16)
     for share in range(out_ref.shape[0]):
-        out_ref[share, :16] = small
-        out_ref[share, 16:] = down
+        out_ref[share] = total
 
 
 def features_kernel(x_ref, low_ref, high_ref, top_ref, bottom_ref, taps_ref, out_ref, flat):
@@ -446,15 +434,15 @@
     channels = cand_ref.shape[0]
     coarse_ch = down_ref.shape[0]
     shares = spread_ref.shape[0]
-    small = spread_ref[:, :16, :].astype(F32)
-    total = (small[:, :8] + small[:, 8:]).reshape(8 * shares, LANES)
+    down_rows = spread_ref.shape[1] - 8
+    total = spread_ref[:, down_rows:, :].astype(F32).reshape(8 * shares, LANES)
     gate_ref[...] = total[: 2 * channels]
     cand_ref[...] = total[2 * channels : 3 * channels, :channels]
     recur_ref[...] = total[2 * channels : 3 * channels, channels:]
     for above in range(3):
         first = 3 * channels + 3 * above
         taps_ref[above] = total[first : first + 3, :channels]
-    down = spread_ref[:, 16:, :].astype(F32).reshape(down_ref.shape[1] // LANES, coarse_ch, LANES)
+    down = spread_ref[:, :down_rows, :].astype(F32).reshape(down_ref.shape[1] // LANES, coarse_ch, LANES)
     for part in range(down.shape[0]):
         down_ref[:, part * LANES : (part + 1) * LANES] = down[part]
 
@@ -536,7 +524,7 @@
     group = (4 * channels, 4 * LANES)
     out_blocks = jax.ShapeDtypeStruct((capacity, coarse_ch + LABEL_ROWS, LANES), BF16)
     down_rows = 16 * channels * coarse_ch // (LANES * shares)
-    packed_shape = jax.ShapeDtypeStruct((shares, 16 + down_rows, LANES), BF16)
+    packed_shape = jax.ShapeDtypeStruct((shares, 8 + down_rows, LANES), BF16)
     everyone = ("range", "azimuth")
 
     pieces = {0: cart_cot.reshape(cot_shape.shape)}
@@ -583,16 +571,18 @@
             pltpu.VMEM(down_weight.shape, F32),
             pltpu.VMEM((ranks,) + out_blocks.shape, BF16),
             pltpu.VMEM((4 * channels, 2 * channels), F32),
-            pltpu.VMEM((9, channels, LANES), F32),
+            pltpu.VMEM((3, channels, 3 * channels), F32),
             flat_scratch,
             pltpu.VMEM((rows // 4 * LANES, 4 * LANES), BF16),
             pltpu.VMEM(down_weight.shape[::-1], BF16),
             pltpu.VMEM((16, LANES), F32),
             pltpu.VMEM((ranks,) + cot_shape.shape, BF16),
+            pltpu.VMEM((slices, 3 * channels, (rows + 2) * LANES), BF16),
+            pltpu.VMEM((channels, rows * LANES), BF16),
             pltpu.SemaphoreType.DMA((ranks,)),
         ],
         name="recur",
-        compiler_params=params(28),
+        compiler_params=params(32),
         cost_estimate=cost(16, 1 << 31),
     )(
         plan,

time: 93.6 us -> 90.4 us (0.966)
  blocking collectives: 17.5 us -> 16.1 us
  waiting for transfers between devices: 14.8 us -> 13.8 us
    all_to_all x1, blocking collectives: 17.5 us -> 16.1 us  [on_device(): pieces = lax.all_to_all(packed, everyone, 0, 0, tiled=True)]
    ppermute x8, waiting for transfers between devices: 14.8 us -> 13.7 us  [shifted(): return lax.ppermute(value, axis, pairs)]
where the time goes in v3:
time: 90.4 us; the launch traced here: 90.1 us
  Pallas kernels  29.3 us (32%)
  starting transfers between devices  28.2 us (31%)
  blocking collectives  16.1 us (18%)
  waiting for transfers between devices  13.8 us (15%)
  local copies, waits for them, and re-layouts  1.91 us (2%)
    pallas_call x1, Pallas kernels, on_device(): pl.pallas_call(functools.partial(recur_kernel, ranks, scale), in_specs=[S...  20.9 us
    ppermute x8, starting transfers between devices, shifted(): return lax.ppermute(value, axis, pairs)  19.5 us
    all_to_all x1, blocking collectives, on_device(): pieces = lax.all_to_all(packed, everyone, 0, 0, tiled=True)  16.1 us
    ppermute x8, waiting for transfers between devices, shifted(): return lax.ppermute(value, axis, pairs)  13.7 us
    pallas_call x1, Pallas kernels, on_device(): pl.pallas_call(features_kernel, in_specs=[VMEM] * 6, out_specs=VMEM, out_...  5.09 us
    all_to_all x1, starting transfers between devices, on_device(): spread = lax.all_to_all(shared, everyone, 0, 0, tiled=True)  2.93 us
    ppermute x3, starting transfers between devices, on_device(): lax.ppermute(outgoing[rank], 'range', [(i, (i + rank) % ranks) for i in r...  2.26 us
    ppermute x1, starting transfers between devices, on_device(): far = lax.ppermute(pieces[0], 'range', [(i, i ^ gap) for i in range(ranks)])  2.09 us
  transfers between devices with their start and end apart: 15, of which 4 were waited for; matrix products, arithmetic and copies ran while one was open for 0% of the time, Pallas kernels for 7%

profile of v3, /device:TPU:1, one launch (start us, length us, event | category | flops | bytes accessed | tf_op | source)
XLA Modules:
  0.0 90.1 jit_solution(5751743024780941237)
XLA Ops:
  0.6 2.1 %collective-permute-start.5 = (bf16[4,128,128]{2,1,0:T(8,128)(2,1)}, bf16[4,128,128]{2,1,0:T(8,128)(2,1)S(1)}, u32[]{:S(2)}, u32[]{:S(2)}) collective-permute-start(bf16[4,128,128]{2,1,0:T(8,128)(2,1)} %bitcast.7), channel_id=1, source_target_pairs={{0,16},{8,24},{16,0},{24,8},{1,17},{9,25},{17,1},{25,9},{2,18},{10... | collective-permute-start | bytes 393224 | tf_op jit(solution)/shard_map/ppermute | solution.py:532
  2.7 1.0 %collective-permute-start.4 = (bf16[4,128,128]{2,1,0:T(8,128)(2,1)}, bf16[4,128,128]{2,1,0:T(8,128)(2,1)S(1)}, u32[]{:S(2)}, u32[]{:S(2)}) collective-permute-start(bf16[4,128,128]{2,1,0:T(8,128)(2,1)} %bitcast.8), channel_id=1, source_target_pairs={{0,8},{8,0},{16,24},{24,16},{1,9},{9,1},{17,25},{25,17},{2,10},{10... | collective-permute-start | bytes 393224 | tf_op jit(solution)/shard_map/ppermute | solution.py:548
  3.7 1.2 %copy-done = bf16[4,64,16,128]{3,2,1,0:T(8,128)(2,1)S(1)} copy-done((bf16[4,64,16,128]{3,2,1,0:T(8,128)(2,1)S(1)}, bf16[4,64,16,128]{3,2,1,0:T(8,128)(2,1)}, u32[]{:S(2)}) %copy-start) | copy-done | bytes 1048600
  4.9 1.1 %split.1 = (bf16[4,16,64,128]{3,2,1,0:T(8,128)(2,1)S(1)}, bf16[4,64,128]{2,1,0:T(8,128)(2,1)S(1)}, bf16[4,64,128]{2,1,0:T(8,128)(2,1)S(1)}) custom-call(bf16[4,64,16,128]{3,2,1,0:T(8,128)(2,1)S(1)} %copy-done), custom_call_target="tpu_custom_call" | custom-call | flops 1048576 | bytes 3145728 | tf_op jit(solution)/shard_map/split/pallas_call | solution.py:533
  6.0 1.3 %collective-permute-start = (bf16[4,64,128]{2,1,0:T(8,128)(2,1)S(1)}, bf16[4,64,128]{2,1,0:T(8,128)(2,1)S(1)}, u32[]{:S(2)}, u32[]{:S(2)}) collective-permute-start(bf16[4,64,128]{2,1,0:T(8,128)(2,1)S(1)} %get-tuple-element.32), channel_id=1, source_target_pairs={{0,1},{1,2},{2,3},{3,4},{4,5},{5,6},{6,7},{7,0},{8,9},{9,10},{10,1... | collective-permute-start | bytes 196616 | tf_op jit(solution)/shard_map/ppermute | solution.py:457
  7.3 3.1 %collective-permute-start.1 = (bf16[4,64,128]{2,1,0:T(8,128)(2,1)S(1)}, bf16[4,64,128]{2,1,0:T(8,128)(2,1)S(1)}, u32[]{:S(2)}, u32[]{:S(2)}) collective-permute-start(bf16[4,64,128]{2,1,0:T(8,128)(2,1)S(1)} %get-tuple-element.33), channel_id=1, source_target_pairs={{1,0},{2,1},{3,2},{4,3},{5,4},{6,5},{7,6},{0,7},{9,8},{10,9},{11,1... | collective-permute-start | bytes 196616 | tf_op jit(solution)/shard_map/ppermute | solution.py:457
  10.9 1.8 %collective-permute-done.low_ref = bf16[4,64,128]{2,1,0:T(8,128)(2,1)S(1)} collective-permute-done((bf16[4,64,128]{2,1,0:T(8,128)(2,1)S(1)}, bf16[4,64,128]{2,1,0:T(8,128)(2,1)S(1)}, u32[]{:S(2)}, u32[]{:S(2)}) %collective-permute-start) | collective-permute-done | bytes 65568 | tf_op jit(solution)/shard_map/ppermute | solution.py:457
  12.8 2.9 %collective-permute-start.2 = (bf16[5,64,128]{2,1,0:T(8,128)(2,1)S(1)}, bf16[5,64,128]{2,1,0:T(8,128)(2,1)S(1)}, u32[]{:S(2)}, u32[]{:S(2)}) collective-permute-start(bf16[5,64,128]{2,1,0:T(8,128)(2,1)S(1)} %get-tuple-element.34), channel_id=1, source_target_pairs={{0,8},{8,16},{16,24},{1,9},{9,17},{17,25},{2,10},{10,18},{18,26},{... | collective-permute-start | bytes 245768 | tf_op jit(solution)/shard_map/ppermute | solution.py:457
  15.7 1.9 %collective-permute-start.3 = (bf16[5,64,128]{2,1,0:T(8,128)(2,1)S(1)}, bf16[5,64,128]{2,1,0:T(8,128)(2,1)S(1)}, u32[]{:S(2)}, u32[]{:S(2)}) collective-permute-start(bf16[5,64,128]{2,1,0:T(8,128)(2,1)S(1)} %get-tuple-element.35), channel_id=1, source_target_pairs={{8,0},{16,8},{24,16},{9,1},{17,9},{25,17},{10,2},{18,10},{26,18},{... | collective-permute-start | bytes 245768 | tf_op jit(solution)/shard_map/ppermute | solution.py:457
  17.7 0.6 copy-done.8
  18.4 3.1 %collective-permute-done.3.bottom_ref = bf16[5,64,128]{2,1,0:T(8,128)(2,1)S(1)} collective-permute-done((bf16[5,64,128]{2,1,0:T(8,128)(2,1)S(1)}, bf16[5,64,128]{2,1,0:T(8,128)(2,1)S(1)}, u32[]{:S(2)}, u32[]{:S(2)}) %collective-permute-start.3) | collective-permute-done | bytes 81952 | tf_op jit(solution)/shard_map/ppermute | solution.py:457
  21.5 20.9 %recur.1 = (bf16[2,144,128]{2,1,0:T(8,128)(2,1)S(1)}, bf16[2,144,128]{2,1,0:T(8,128)(2,1)S(1)}, bf16[2,144,128]{2,1,0:T(8,128)(2,1)S(1)}, bf16[2,144,128]{2,1,0:...) custom-call(s32[9]{0:T(128)S(1)} %pad_add_fusion.plan, ...), custom_call_target="tpu_custom_call" | custom-call | flops 2147483648 | bytes 16777216 | tf_op jit(solution)/shard_map/recur/pallas_call | solution.py:552
  42.4 16.1 %all_to_all.10.pieces_ref = bf16[32,40,128]{2,1,0:T(8,128)(2,1)S(1)} all-to-all(bf16[32,40,128]{2,1,0:T(8,128)(2,1)S(1)} %get-tuple-element.36), channel_id=1, replica_groups=mesh['range'=4,'azimuth'=8] {'range','azimuth'}, dimensions={0} | all-to-all | bytes 655360 | tf_op jit(solution)/shard_map/all_to_all | solution.py:597
  58.5 0.8 share.1
  59.3 2.9 %all-to-all-start.1 = ((bf16[32,40,128]{2,1,0:T(8,128)(2,1)}), bf16[32,40,128]{2,1,0:T(8,128)(2,1)S(1)}, u32[]{:S(2)}, u32[]{:S(2)}) async-start(bf16[32,40,128]{2,1,0:T(8,128)(2,1)} %share.1), calls=%async_computation.1 | async-start | bytes 655360 | tf_op jit(solution)/shard_map/all_to_all | solution.py:612
  62.2 1.4 %collective-permute-start.10 = (bf16[4,64,128]{2,1,0:T(8,128)(2,1)S(1)}, bf16[4,64,128]{2,1,0:T(8,128)(2,1)S(1)}, u32[]{:S(2)}, u32[]{:S(2)}) collective-permute-start(bf16[4,64,128]{2,1,0:T(8,128)(2,1)S(1)} %get-tuple-element.43), channel_id=1, source_target_pairs={{0,1},{1,2},{2,3},{3,4},{4,5},{5,6},{6,7},{7,0},{8,9},{9,10},{10,1... | collective-permute-start | bytes 196616 | tf_op jit(solution)/shard_map/ppermute | solution.py:457
  63.7 3.0 %collective-permute-start.11 = (bf16[4,64,128]{2,1,0:T(8,128)(2,1)S(1)}, bf16[4,64,128]{2,1,0:T(8,128)(2,1)S(1)}, u32[]{:S(2)}, u32[]{:S(2)}) collective-permute-start(bf16[4,64,128]{2,1,0:T(8,128)(2,1)S(1)} %get-tuple-element.44), channel_id=1, source_target_pairs={{1,0},{2,1},{3,2},{4,3},{5,4},{6,5},{7,6},{0,7},{9,8},{10,9},{11,1... | collective-permute-start | bytes 196616 | tf_op jit(solution)/shard_map/ppermute | solution.py:457
  66.6 7.3 %collective-permute-done.10.low_ref = bf16[4,64,128]{2,1,0:T(8,128)(2,1)S(1)} collective-permute-done((bf16[4,64,128]{2,1,0:T(8,128)(2,1)S(1)}, bf16[4,64,128]{2,1,0:T(8,128)(2,1)S(1)}, u32[]{:S(2)}, u32[]{:S(2)}) %collective-permute-start.10) | collective-permute-done | bytes 65568 | tf_op jit(solution)/shard_map/ppermute | solution.py:457
  74.1 4.0 %collective-permute-start.12 = (bf16[5,64,128]{2,1,0:T(8,128)(2,1)S(1)}, bf16[5,64,128]{2,1,0:T(8,128)(2,1)S(1)}, u32[]{:S(2)}, u32[]{:S(2)}) collective-permute-start(bf16[5,64,128]{2,1,0:T(8,128)(2,1)S(1)} %get-tuple-element.45), channel_id=1, source_target_pairs={{0,8},{8,16},{16,24},{1,9},{9,17},{17,25},{2,10},{10,18},{18,26},{... | collective-permute-start | bytes 245768 | tf_op jit(solution)/shard_map/ppermute | solution.py:457
  78.1 1.9 %collective-permute-start.13 = (bf16[5,64,128]{2,1,0:T(8,128)(2,1)S(1)}, bf16[5,64,128]{2,1,0:T(8,128)(2,1)S(1)}, u32[]{:S(2)}, u32[]{:S(2)}) collective-permute-start(bf16[5,64,128]{2,1,0:T(8,128)(2,1)S(1)} %get-tuple-element.46), channel_id=1, source_target_pairs={{8,0},{16,8},{24,16},{9,1},{17,9},{25,17},{10,2},{18,10},{26,18},{... | collective-permute-start | bytes 245768 | tf_op jit(solution)/shard_map/ppermute | solution.py:457
  80.0 1.8 %collective-permute-start.7 = (bf16[2,144,128]{2,1,0:T(8,128)(2,1)S(1)}, bf16[2,144,128]{2,1,0:T(8,128)(2,1)S(1)}, u32[]{:S(2)}, u32[]{:S(2)}) collective-permute-start(bf16[2,144,128]{2,1,0:T(8,128)(2,1)S(1)} %get-tuple-element.38), channel_id=1, source_target_pairs={{0,8},{8,16},{16,24},{24,0},{1,9},{9,17},{17,25},{25,1},{2,10},{10... | collective-permute-start | bytes 221192 | tf_op jit(solution)/shard_map/ppermute | solution.py:600
  82.3 1.6 %collective-permute-done.13.bottom_ref = bf16[5,64,128]{2,1,0:T(8,128)(2,1)S(1)} collective-permute-done((bf16[5,64,128]{2,1,0:T(8,128)(2,1)S(1)}, bf16[5,64,128]{2,1,0:T(8,128)(2,1)S(1)}, u32[]{:S(2)}, u32[]{:S(2)}) %collective-permute-start.13) | collective-permute-done | bytes 81952 | tf_op jit(solution)/shard_map/ppermute | solution.py:457
  83.8 5.1 %features.1 = bf16[4,64,16,128]{3,2,1,0:T(8,128)(2,1)} custom-call(bf16[4,16,64,128]{3,2,1,0:T(8,128)(2,1)S(1)} %get-tuple-element.42.rows_ref.x_ref, bf16[4,64,128]{2,1,0:T(8,128)(2,1)S(1)} %collective-permute-done.10.low_ref, bf16[4,64,128]{2,1,0:T(8,128)(2,1)S(1)} %collective-permute-done.11.high_ref, ...), custom_call_target="tpu_custom_call" | custom-call | flops 33554432 | bytes 4194304 | tf_op jit(solution)/shard_map/features/pallas_call | solution.py:613
  88.9 1.1 %finish.1 = (f32[128,128]{1,0:T(8,128)}, f32[64,64]{1,0:T(8,128)}, f32[64,64]{1,0:T(8,128)}, f32[3,3,64]{2,1,0:T(4,128)}, f32[128,1024]{1,0:T(8,128)}, /*index=5*/f32[4,128,128]{2,1,0:T(8,128)}) custom-call(bf16[32,40,128]{2,1,0:T(8,128)(2,1)S(1)} %all-to-all-done.1.spread_ref, bf16[2,144,128]{2,1,0:T(8,128)(2,1)S(1)} %get-tuple-element.37.refs_0_, ...), custom_call_target="tpu_custom_call" | custom-call | flops 1048576 | bytes 1048576 | tf_op jit(solution)/shard_map/finish/pallas_call | solution.py:623
  (36 shorter events, 1.4 us)
Async XLA Ops:
  0.6 9.8 %collective-permute-start.5 = (bf16[4,128,128]{2,1,0:T(8,128)(2,1)}, bf16[4,128,128]{2,1,0:T(8,128)(2,1)S(1)}, u32[]{:S(2)}, u32[]{:S(2)}) collective-permute-start(bf16[4,128,128]{2,1,0:T(8,128)(2,1)} %bitcast.7), channel_id=1, source_target_pairs={{0,16},{8,24},{16,0},{24,8},{1,17},{9,25},{17,1},{25,9},{2,18},{10... | collective-permute-start | bytes 393224 | tf_op jit(solution)/shard_map/ppermute | solution.py:532
  2.7 15.7 %collective-permute-start.4 = (bf16[4,128,128]{2,1,0:T(8,128)(2,1)}, bf16[4,128,128]{2,1,0:T(8,128)(2,1)S(1)}, u32[]{:S(2)}, u32[]{:S(2)}) collective-permute-start(bf16[4,128,128]{2,1,0:T(8,128)(2,1)} %bitcast.8), channel_id=1, source_target_pairs={{0,8},{8,0},{16,24},{24,16},{1,9},{9,1},{17,25},{25,17},{2,10},{10... | collective-permute-start | bytes 393224 | tf_op jit(solution)/shard_map/ppermute | solution.py:548
  3.7 1.2 %copy-start = (bf16[4,64,16,128]{3,2,1,0:T(8,128)(2,1)S(1)}, bf16[4,64,16,128]{3,2,1,0:T(8,128)(2,1)}, u32[]{:S(2)}) copy-start(bf16[4,64,16,128]{3,2,1,0:T(8,128)(2,1)} %x_ref.1) | copy-start | bytes 3145732
  4.9 5.9 %copy-start.5 = (bf16[128,128]{1,0:T(8,128)(2,1)S(1)}, bf16[128,128]{1,0:T(8,128)(2,1)}, u32[]{:S(2)}) copy-start(bf16[128,128]{1,0:T(8,128)(2,1)} %param.13) | copy-start | bytes 98308
  4.9 5.9 %copy-start.6 = (bf16[64,64]{1,0:T(8,128)(2,1)S(1)}, bf16[64,64]{1,0:T(8,128)(2,1)}, u32[]{:S(2)}) copy-start(bf16[64,64]{1,0:T(8,128)(2,1)} %param.15) | copy-start | bytes 24580
  4.9 5.9 %copy-start.7 = (bf16[64,64]{1,0:T(8,128)(2,1)S(1)}, bf16[64,64]{1,0:T(8,128)(2,1)}, u32[]{:S(2)}) copy-start(bf16[64,64]{1,0:T(8,128)(2,1)} %param.14) | copy-start | bytes 24580
  6.0 6.6 %collective-permute-start = (bf16[4,64,128]{2,1,0:T(8,128)(2,1)S(1)}, bf16[4,64,128]{2,1,0:T(8,128)(2,1)S(1)}, u32[]{:S(2)}, u32[]{:S(2)}) collective-permute-start(bf16[4,64,128]{2,1,0:T(8,128)(2,1)S(1)} %get-tuple-element.32), channel_id=1, source_target_pairs={{0,1},{1,2},{2,3},{3,4},{4,5},{5,6},{6,7},{7,0},{8,9},{9,10},{10,1... | collective-permute-start | bytes 196616 | tf_op jit(solution)/shard_map/ppermute | solution.py:457
  7.3 5.3 %collective-permute-start.1 = (bf16[4,64,128]{2,1,0:T(8,128)(2,1)S(1)}, bf16[4,64,128]{2,1,0:T(8,128)(2,1)S(1)}, u32[]{:S(2)}, u32[]{:S(2)}) collective-permute-start(bf16[4,64,128]{2,1,0:T(8,128)(2,1)S(1)} %get-tuple-element.33), channel_id=1, source_target_pairs={{1,0},{2,1},{3,2},{4,3},{5,4},{6,5},{7,6},{0,7},{9,8},{10,9},{11,1... | collective-permute-start | bytes 196616 | tf_op jit(solution)/shard_map/ppermute | solution.py:457
  10.4 11.1 %collective-permute-start.6 = (bf16[4,128,128]{2,1,0:T(8,128)(2,1)S(1)}, bf16[4,128,128]{2,1,0:T(8,128)(2,1)S(1)}, u32[]{:S(2)}, u32[]{:S(2)}) collective-permute-start(bf16[4,128,128]{2,1,0:T(8,128)(2,1)S(1)} %collective-permute-done.5.rest_2_), channel_id=1, source_target_pairs={{0,8},{8,0},{16,24},{24,16},{1,9},{9,1},{17,25},{25,17},{2,10},{10... | collective-permute-start | bytes 393224 | tf_op jit(solution)/shard_map/ppermute | solution.py:548
  12.7 8.9 %copy-start.1 = (bf16[64,16,128]{2,1,0:T(8,128)(2,1)S(1)}, bf16[64,16,128]{2,1,0:T(8,128)(2,1)}, u32[]{:S(2)}) copy-start(bf16[64,16,128]{2,1,0:T(8,128)(2,1)} %state_ref.1) | copy-start | bytes 786436
  12.7 8.9 %copy-start.2 = (bf16[128,1024]{1,0:T(8,128)(2,1)S(1)}, bf16[128,1024]{1,0:T(8,128)(2,1)}, u32[]{:S(2)}) copy-start(bf16[128,1024]{1,0:T(8,128)(2,1)} %down_ref.1) | copy-start | bytes 786436
  12.7 8.9 %copy-start.3 = (bf16[1,1,4,128,128]{4,3,2,1,0:T(8,128)(2,1)S(1)}, bf16[1,1,4,128,128]{4,3,2,1,0:T(8,128)(2,1)}, u32[]{:S(2)}) copy-start(bf16[1,1,4,128,128]{4,3,2,1,0:T(8,128)(2,1)} %param.19) | copy-start | bytes 393220
  12.8 8.7 %copy-start.4 = (f32[64,3,3]{0,2,1:T(4,128)S(1)}, f32[64,3,3]{0,2,1:T(4,128)}, u32[]{:S(2)}) copy-start(f32[64,3,3]{0,2,1:T(4,128)} %param.12) | copy-start | bytes 6916
  12.8 5.6 %collective-permute-start.2 = (bf16[5,64,128]{2,1,0:T(8,128)(2,1)S(1)}, bf16[5,64,128]{2,1,0:T(8,128)(2,1)S(1)}, u32[]{:S(2)}, u32[]{:S(2)}) collective-permute-start(bf16[5,64,128]{2,1,0:T(8,128)(2,1)S(1)} %get-tuple-element.34), channel_id=1, source_target_pairs={{0,8},{8,16},{16,24},{1,9},{9,17},{17,25},{2,10},{10,18},{18,26},{... | collective-permute-start | bytes 245768 | tf_op jit(solution)/shard_map/ppermute | solution.py:457
  15.7 5.8 %collective-permute-start.3 = (bf16[5,64,128]{2,1,0:T(8,128)(2,1)S(1)}, bf16[5,64,128]{2,1,0:T(8,128)(2,1)S(1)}, u32[]{:S(2)}, u32[]{:S(2)}) collective-permute-start(bf16[5,64,128]{2,1,0:T(8,128)(2,1)S(1)} %get-tuple-element.35), channel_id=1, source_target_pairs={{8,0},{16,8},{24,16},{9,1},{17,9},{25,17},{10,2},{18,10},{26,18},{... | collective-permute-start | bytes 245768 | tf_op jit(solution)/shard_map/ppermute | solution.py:457
  17.7 0.7 copy-start.9
  59.3 29.6 %all-to-all-start.1 = ((bf16[32,40,128]{2,1,0:T(8,128)(2,1)}), bf16[32,40,128]{2,1,0:T(8,128)(2,1)S(1)}, u32[]{:S(2)}, u32[]{:S(2)}) async-start(bf16[32,40,128]{2,1,0:T(8,128)(2,1)} %share.1), calls=%async_computation.1 | async-start | bytes 655360 | tf_op jit(solution)/shard_map/all_to_all | solution.py:612
  62.2 11.7 %collective-permute-start.10 = (bf16[4,64,128]{2,1,0:T(8,128)(2,1)S(1)}, bf16[4,64,128]{2,1,0:T(8,128)(2,1)S(1)}, u32[]{:S(2)}, u32[]{:S(2)}) collective-permute-start(bf16[4,64,128]{2,1,0:T(8,128)(2,1)S(1)} %get-tuple-element.43), channel_id=1, source_target_pairs={{0,1},{1,2},{2,3},{3,4},{4,5},{5,6},{6,7},{7,0},{8,9},{9,10},{10,1... | collective-permute-start | bytes 196616 | tf_op jit(solution)/shard_map/ppermute | solution.py:457
  63.7 10.3 %collective-permute-start.11 = (bf16[4,64,128]{2,1,0:T(8,128)(2,1)S(1)}, bf16[4,64,128]{2,1,0:T(8,128)(2,1)S(1)}, u32[]{:S(2)}, u32[]{:S(2)}) collective-permute-start(bf16[4,64,128]{2,1,0:T(8,128)(2,1)S(1)} %get-tuple-element.44), channel_id=1, source_target_pairs={{1,0},{2,1},{3,2},{4,3},{5,4},{6,5},{7,6},{0,7},{9,8},{10,9},{11,1... | collective-permute-start | bytes 196616 | tf_op jit(solution)/shard_map/ppermute | solution.py:457
  74.1 8.2 %collective-permute-start.12 = (bf16[5,64,128]{2,1,0:T(8,128)(2,1)S(1)}, bf16[5,64,128]{2,1,0:T(8,128)(2,1)S(1)}, u32[]{:S(2)}, u32[]{:S(2)}) collective-permute-start(bf16[5,64,128]{2,1,0:T(8,128)(2,1)S(1)} %get-tuple-element.45), channel_id=1, source_target_pairs={{0,8},{8,16},{16,24},{1,9},{9,17},{17,25},{2,10},{10,18},{18,26},{... | collective-permute-start | bytes 245768 | tf_op jit(solution)/shard_map/ppermute | solution.py:457
  78.1 5.8 %collective-permute-start.13 = (bf16[5,64,128]{2,1,0:T(8,128)(2,1)S(1)}, bf16[5,64,128]{2,1,0:T(8,128)(2,1)S(1)}, u32[]{:S(2)}, u32[]{:S(2)}) collective-permute-start(bf16[5,64,128]{2,1,0:T(8,128)(2,1)S(1)} %get-tuple-element.46), channel_id=1, source_target_pairs={{8,0},{16,8},{24,16},{9,1},{17,9},{25,17},{10,2},{18,10},{26,18},{... | collective-permute-start | bytes 245768 | tf_op jit(solution)/shard_map/ppermute | solution.py:457
  80.0 8.9 %collective-permute-start.7 = (bf16[2,144,128]{2,1,0:T(8,128)(2,1)S(1)}, bf16[2,144,128]{2,1,0:T(8,128)(2,1)S(1)}, u32[]{:S(2)}, u32[]{:S(2)}) collective-permute-start(bf16[2,144,128]{2,1,0:T(8,128)(2,1)S(1)} %get-tuple-element.38), channel_id=1, source_target_pairs={{0,8},{8,16},{16,24},{24,0},{1,9},{9,17},{17,25},{25,1},{2,10},{10... | collective-permute-start | bytes 221192 | tf_op jit(solution)/shard_map/ppermute | solution.py:600
  81.8 7.1 %collective-permute-start.8 = (bf16[2,144,128]{2,1,0:T(8,128)(2,1)S(1)}, bf16[2,144,128]{2,1,0:T(8,128)(2,1)S(1)}, u32[]{:S(2)}, u32[]{:S(2)}) collective-permute-start(bf16[2,144,128]{2,1,0:T(8,128)(2,1)S(1)} %get-tuple-element.39), channel_id=1, source_target_pairs={{0,16},{8,24},{16,0},{24,8},{1,17},{9,25},{17,1},{25,9},{2,18},{10... | collective-permute-start | bytes 221192 | tf_op jit(solution)/shard_map/ppermute | solution.py:600
  81.8 7.1 %collective-permute-start.9 = (bf16[2,144,128]{2,1,0:T(8,128)(2,1)S(1)}, bf16[2,144,128]{2,1,0:T(8,128)(2,1)S(1)}, u32[]{:S(2)}, u32[]{:S(2)}) collective-permute-start(bf16[2,144,128]{2,1,0:T(8,128)(2,1)S(1)} %get-tuple-element.40), channel_id=1, source_target_pairs={{0,24},{8,0},{16,8},{24,16},{1,25},{9,1},{17,9},{25,17},{2,26},{10... | collective-permute-start | bytes 221192 | tf_op jit(solution)/shard_map/ppermute | solution.py:600
  (1 other events, 0.7 us)
